TPU v7x, 32 devices: a whole 2x2x4 slice. The times are simulated.
32 devices in a mesh: expert: 16 (over z, y, x), mp: 2 (over core).
Axes of the slice: x: 2, y: 2, z: 4, core: 2. Of those that a mesh axis runs over, the one named last changes fastest.
Arguments:
- tokens: bfloat16 [2048, 2048], P('expert', 'mp'), may hold values from -6 to 6
- expert_ids: int32 [2048, 2], P('expert'), may hold values from 0 to 15, all different within a row; in each aligned block of 128 rows (0 to 127, 128 to 255, ...) at most 32 rows name the same one
- combine: float32 [2048, 2], P('expert'), may hold values from 0.2 to 1
- w_gate: bfloat16 [16, 2048, 2048], P('expert', None, 'mp'), may hold values from -0.125 to 0.125
- w_up: bfloat16 [16, 2048, 2048], P('expert', None, 'mp'), may hold values from -0.125 to 0.125
- w_down: bfloat16 [16, 2048, 2048], P('expert', 'mp'), may hold values from -0.125 to 0.125
- grad_out: bfloat16 [2048, 2048], P('expert', 'mp'), may hold values from -6 to 6
Outputs:
- output: bfloat16 [2048, 2048], P('expert', 'mp')
- grad_tokens: bfloat16 [2048, 2048], P('expert', 'mp')
- grad_down: bfloat16 [16, 2048, 2048], P('expert', 'mp')
Inputs may be any that keep to these rules, and one draw needn't show every extreme that they name: `expert_ids`: the ids of a row differ. In each aligned block of 128 rows (the rows of one index of expert) no expert is named by more than 32 rows, and in every draw some block names some expert exactly 32 times.
All inputs are finite; a program needn't handle non-finite values.
Results may differ from a plain program's by a relative error of at most 0.015.
Values may be sent and summed in bfloat16 or wider, within the bound.
No kernel may reach another device: no remote copies, remote signals or barrier semaphores. Data moves between devices by JAX's collectives and lax.ppermute only.
A program may use at most 64 MiB of HBM per device.

v0:
```python
import jax
import jax.numpy as jnp
from jax import lax
from jax.sharding import PartitionSpec as P


def pick_rows(source, source_row, row_scale):
    picked_rows = jnp.take(source, source_row, axis=0)
    return (picked_rows.astype(jnp.float32) * row_scale[:, None]).astype(jnp.bfloat16)


def arrive(local_rows, source_row, row_scale):
    whole_rows = lax.all_gather(local_rows, "mp", axis=1, tiled=True)
    arrived = lax.all_to_all(
        pick_rows(whole_rows, source_row, row_scale),
        "expert",
        split_axis=0,
        concat_axis=0,
        tiled=True,
    )
    return arrived


def depart(partial_sum, slot_index, pick_weight, row_count, top_count):
    shares = lax.psum_scatter(
        partial_sum.astype(jnp.bfloat16), "mp", scatter_dimension=1, tiled=True
    ).astype(jnp.float32)
    returned = lax.all_to_all(
        shares.astype(jnp.bfloat16), "expert", split_axis=0, concat_axis=0, tiled=True
    ).astype(shares.dtype)
    gathered = jnp.take(returned, slot_index, axis=0).reshape(row_count, top_count, -1)
    combined = jnp.sum(gathered * pick_weight[:, :, None], axis=1)
    return combined.astype(jnp.bfloat16)


def shards(tokens, expert_ids, combine, w_gate, w_up, w_down, grad_out):
    row_count = tokens.shape[0]
    top_count = expert_ids.shape[1]
    expert_count = lax.axis_size("expert")
    most_slots = 4 * row_count // expert_count
    slot_total = expert_count * most_slots
    pick_count = row_count * top_count
    w_gate_local = w_gate[0]
    w_up_local = w_up[0]
    w_down_local = w_down[0]
    flat_ids = expert_ids.reshape(-1)
    onehot = (flat_ids[:, None] == jnp.arange(expert_count, dtype=jnp.int32)[None, :]).astype(
        jnp.int32
    )
    earlier = jnp.cumsum(onehot, axis=0) - onehot
    rank_within = jnp.sum(earlier * onehot, axis=1)
    slot_index = flat_ids * most_slots + rank_within
    filler = (
        jnp.full((slot_total,), pick_count, jnp.int32)
        .at[slot_index]
        .set(jnp.arange(pick_count, dtype=jnp.int32))
    )
    slot_used = filler < pick_count
    safe_pick = jnp.where(slot_used, filler, 0)
    source_row = safe_pick // top_count
    forward_scale = slot_used.astype(jnp.float32)
    backward_scale = jnp.where(slot_used, combine.reshape(-1)[safe_pick], jnp.float32(0.0))
    arrived_rows = arrive(tokens, source_row, forward_scale)
    gate_value = jnp.dot(arrived_rows, w_gate_local, preferred_element_type=jnp.float32)
    up_value = jnp.dot(arrived_rows, w_up_local, preferred_element_type=jnp.float32)
    sigmoid_gate = jax.nn.sigmoid(gate_value)
    hidden = (gate_value * sigmoid_gate * up_value).astype(jnp.bfloat16)
    out_partial = jnp.dot(hidden, w_down_local, preferred_element_type=jnp.float32)
    output = depart(out_partial, slot_index, combine, row_count, top_count)
    arrived_grads = arrive(grad_out, source_row, backward_scale)
    grad_hidden = lax.dot_general(
        arrived_grads, w_down_local, (((1,), (1,)), ((), ())), preferred_element_type=jnp.float32
    )
    down_grad = lax.dot_general(
        hidden, arrived_grads, (((0,), (0,)), ((), ())), preferred_element_type=jnp.float32
    )
    grad_up = (grad_hidden * gate_value * sigmoid_gate).astype(jnp.bfloat16)
    grad_gate = (
        grad_hidden * up_value * sigmoid_gate * (1.0 + gate_value * (1.0 - sigmoid_gate))
    ).astype(jnp.bfloat16)
    grad_terms = lax.dot_general(
        grad_gate, w_gate_local, (((1,), (1,)), ((), ())), preferred_element_type=jnp.float32
    )
    grad_terms = grad_terms + lax.dot_general(
        grad_up, w_up_local, (((1,), (1,)), ((), ())), preferred_element_type=jnp.float32
    )
    unit_weight = jnp.ones((row_count, top_count), jnp.float32)
    grad_tokens = depart(grad_terms, slot_index, unit_weight, row_count, top_count)
    return (output, grad_tokens, down_grad.astype(jnp.bfloat16)[None])


def solution(mesh):
    return jax.shard_map(
        shards,
        mesh=mesh,
        in_specs=(
            P("expert", "mp"),
            P("expert", None),
            P("expert", None),
            P("expert", None, "mp"),
            P("expert", None, "mp"),
            P("expert", "mp", None),
            P("expert", "mp"),
        ),
        out_specs=(P("expert", "mp"), P("expert", "mp"), P("expert", "mp", None)),
        check_vma=False,
    )
```

profile of v0, /device:TPU:8, one launch (start us, length us, event | category | flops | bytes accessed | tf_op | source)
XLA Modules:
  0.0 242.3 jit_solution(14807136436938609058)
XLA Ops:
  7.2 0.7 broadcast_multiply_fusion
  7.9 0.8 copy.11
  8.7 0.1 eq.25
  8.8 0.1 eq.29
  9.0 0.1 copy.14
  9.1 0.1 mul.73
  9.2 0.6 reduce-window.6
  9.8 0.2 slice_reduce_fusion
  10.1 0.1 fusion.21
  10.2 1.4 scatter_custom_fusion
  11.6 2.4 all_gather.7
  14.0 0.8 copy.15
  14.8 0.1 reshape.88
  14.9 3.5 %gather_fusion = f32[512]{0:T(512)S(1)} fusion(f32[256]{0:T(256)S(1)} %reshape.88, s32[1024]{0:T(1024)S(1)} %pad_clamp_fusion), kind=kCustom, calls=%fused_computation.4 | custom fusion | bytes 6144 | tf_op jit(solution)/shard_map/gather | solution.py:62
  18.5 2.2 all_gather.6
  20.7 2.5 %gather_fusion.3 = bf16[512,2048]{1,0:T(8,128)(2,1)S(1)} fusion(bf16[128,2048]{1,0:T(8,128)(2,1)S(1)} %all_gather.7, s32[1024]{0:T(1024)S(1)} %pad_clamp_fusion.2), kind=kCustom, calls=%fused_computation.2.clone | custom fusion | bytes 4196352 | tf_op jit(solution)/shard_map/jit(_take)/gather | solution.py:8
  23.1 3.3 %gather_fusion.1 = bf16[512,2048]{1,0:T(8,128)(2,1)} fusion(bf16[128,2048]{1,0:T(8,128)(2,1)S(1)} %all_gather.6, s32[1024]{0:T(1024)S(1)} %pad_clamp_fusion.2), kind=kCustom, calls=%fused_computation.clone | custom fusion | bytes 4196352 | tf_op jit(solution)/shard_map/jit(_take)/gather | solution.py:8
  26.4 3.3 %multiply_convert_fusion = (bf16[512,2048]{1,0:T(8,128)(2,1)S(1)}, bf16[512,2048]{1,0:T(8,128)(2,1)}) fusion(bf16[512,2048]{1,0:T(8,128)(2,1)S(1)} %gather_fusion.3, f32[512]{0:T(512)S(1)} %broadcast_select_fusion.2, pred[512]{0:T(512)(128)(4,1)S(1)} %get-tuple-element.7, f32[512]{0:T(512)S(1)} %get-tuple-element.9, bf16[512,2048]{1,0:T(8,128)(2,1)} %gather_fusion.1), kind=kLoop, calls=%fused_computation.20 | loop fusion | flops 8388608 | bytes 8393216 | tf_op jit(solution)/shard_map/convert_element_type | solution.py:9
  29.7 55.5 %all_to_all.42 = bf16[16,32,2048]{2,1,0:T(8,128)(2,1)S(1)} all-to-all(bf16[16,32,2048]{2,1,0:T(8,128)(2,1)S(1)} %bitcast.62), channel_id=1, replica_groups=mesh['expert'=16,'mp'=2] {'expert'}, dimensions={0} | all-to-all | bytes 4194304 | tf_op jit(solution)/shard_map/all_to_all | solution.py:14
  85.2 4.9 %all-to-all-start = ((bf16[16,32,2048]{2,1,0:T(8,128)(2,1)}), bf16[16,32,2048]{2,1,0:T(8,128)(2,1)}, u32[]{:S(2)}, u32[]{:S(2)}) async-start(bf16[16,32,2048]{2,1,0:T(8,128)(2,1)} %bitcast.3), calls=%async_computation | async-start | bytes 4194304 | tf_op jit(solution)/shard_map/all_to_all | solution.py:14
  90.1 0.2 reduce-scatter.5.cloned.1.call-start
  90.3 5.9 %fusion = f32[512,1024]{1,0:T(8,128)} fusion(bf16[512,2048]{1,0:T(8,128)(2,1)S(1)} %bitcast.63, bf16[1,1024,2048]{2,1,0:T(8,128)(2,1)} %param.16), kind=kOutput, calls=%fused_computation.6 | convolution fusion | flops 2147483648 | bytes 8388608 | tf_op jit(solution)/shard_map/dot_general | solution.py:71
  96.1 40.5 %all-to-all-done = bf16[16,32,2048]{2,1,0:T(8,128)(2,1)} async-done(((bf16[16,32,2048]{2,1,0:T(8,128)(2,1)}), bf16[16,32,2048]{2,1,0:T(8,128)(2,1)}, u32[]{:S(2)}, u32[]{:S(2)}) %all-to-all-start) | async-done | bytes 2097184 | tf_op jit(solution)/shard_map/all_to_all | solution.py:14
  136.6 5.3 %fusion.10 = f32[512,1024]{1,0:T(8,128)S(1)} fusion(bf16[512,2048]{1,0:T(8,128)(2,1)} %bitcast.4, bf16[1,2048,1024]{2,1,0:T(8,128)(2,1)} %param.14), kind=kOutput, calls=%fused_computation.16 | convolution fusion | flops 2147483648 | bytes 8388608 | tf_op jit(solution)/shard_map/dot_general | solution.py:64
  142.0 4.3 %multiply_convert_fusion.4 = (bf16[512,1024]{1,0:T(8,128)(2,1)S(1)}, f32[512,1024]{1,0:T(8,128)S(1)}) fusion(f32[512,1024]{1,0:T(8,128)S(1)} %fusion.10, bf16[512,2048]{1,0:T(8,128)(2,1)} %bitcast.4, bf16[1,2048,1024]{2,1,0:T(8,128)(2,1)S(1)} %copy-done.1), kind=kOutput, calls=%fused_computation.25 | convolution fusion | flops 2150629376 | bytes 11534336 | tf_op jit(solution)/shard_map/dot_general | solution.py:65
  146.3 2.4 fusion.4
  148.7 0.1 copy-done.2
  148.8 4.2 %add_convert_fusion = bf16[512,2048]{1,0:T(8,128)(2,1)} fusion(f32[512,2048]{1,0:T(8,128)S(1)} %fusion.4, bf16[1,2048,1024]{2,1,0:T(8,128)(2,1)S(1)} %copy-done.2, f32[512,1024]{1,0:T(8,128)S(1)} %fusion.10, f32[512,1024]{1,0:T(8,128)S(1)} %copy-done.3, f32[512,1024]{1,0:T(8,128)S(1)} %get-tuple-element.15), kind=kOutput, calls=%fused_computation.19 | convolution fusion | flops 2154823680 | bytes 16777216 | tf_op jit(solution)/shard_map/dot_general | solution.py:81
  153.0 0.0 reduce-scatter.5.cloned.1.call-update
  153.1 0.0 reduce-scatter.3.cloned.1.call-start
  153.1 5.9 %fusion.14 = bf16[512,2048]{1,0:T(8,128)(2,1)} fusion(bf16[512,1024]{1,0:T(8,128)(2,1)S(1)} %get-tuple-element.14, bf16[1,1024,2048]{2,1,0:T(8,128)(2,1)} %param.16), kind=kOutput, calls=%fused_computation.22 | convolution fusion | flops 2148532224 | bytes 7340032 | tf_op jit(solution)/shard_map/dot_general | solution.py:68
  159.0 0.0 reduce-scatter.3.cloned.1.call-update
  159.0 3.8 %reduce-scatter.5.cloned.1.call-done = bf16[512,1024]{1,0:T(8,128)(2,1)} async-done(((bf16[512,2048]{1,0:T(8,128)(2,1)}), bf16[512,1024]{1,0:T(8,128)(2,1)}) %reduce-scatter.5.cloned.1.call-update) | async-done | bytes 1048592 | tf_op jit(solution)/shard_map/reduce_scatter | solution.py:25
  162.8 7.0 %all-to-all-start.3 = ((bf16[16,32,1024]{2,1,0:T(8,128)(2,1)}), bf16[16,32,1024]{2,1,0:T(8,128)(2,1)S(1)}, u32[]{:S(2)}, u32[]{:S(2)}) async-start(bf16[16,32,1024]{2,1,0:T(8,128)(2,1)} %bitcast.66), calls=%async_computation.5 | async-start | bytes 2097152 | tf_op jit(solution)/shard_map/all_to_all | solution.py:28
  169.8 6.2 %reduce-scatter.3.cloned.1.call-done = bf16[512,1024]{1,0:T(8,128)(2,1)} async-done(((bf16[512,2048]{1,0:T(8,128)(2,1)}), bf16[512,1024]{1,0:T(8,128)(2,1)}) %reduce-scatter.3.cloned.1.call-update) | async-done | bytes 1048592 | tf_op jit(solution)/shard_map/reduce_scatter | solution.py:25
  176.0 19.5 %all-to-all-done.3 = bf16[16,32,1024]{2,1,0:T(8,128)(2,1)S(1)} async-done(((bf16[16,32,1024]{2,1,0:T(8,128)(2,1)}), bf16[16,32,1024]{2,1,0:T(8,128)(2,1)S(1)}, u32[]{:S(2)}, u32[]{:S(2)}) %all-to-all-start.3) | async-done | bytes 1048608 | tf_op jit(solution)/shard_map/all_to_all | solution.py:28
  195.5 5.1 %all-to-all-start.1 = ((bf16[16,32,1024]{2,1,0:T(8,128)(2,1)}), bf16[16,32,1024]{2,1,0:T(8,128)(2,1)}, u32[]{:S(2)}, u32[]{:S(2)}) async-start(bf16[16,32,1024]{2,1,0:T(8,128)(2,1)} %bitcast.65), calls=%async_computation.2 | async-start | bytes 2097152 | tf_op jit(solution)/shard_map/all_to_all | solution.py:28
  200.6 5.6 %convert_bitcast_fusion = bf16[1,1024,2048]{2,1,0:T(8,128)(2,1)} fusion(bf16[512,1024]{1,0:T(8,128)(2,1)} %copy-done.4, bf16[512,2048]{1,0:T(8,128)(2,1)S(1)} %bitcast.64), kind=kOutput, calls=%fused_computation.18 | convolution fusion | flops 2149580800 | bytes 7340032 | tf_op jit(solution)/shard_map/dot_general | solution.py:74
  206.3 0.3 bitcast_convert_fusion
  206.6 1.1 gather_fusion.4
  207.7 17.5 %all-to-all-done.1 = bf16[16,32,1024]{2,1,0:T(8,128)(2,1)} async-done(((bf16[16,32,1024]{2,1,0:T(8,128)(2,1)}), bf16[16,32,1024]{2,1,0:T(8,128)(2,1)}, u32[]{:S(2)}, u32[]{:S(2)}) %all-to-all-start.1) | async-done | bytes 1048608 | tf_op jit(solution)/shard_map/all_to_all | solution.py:28
  225.2 1.5 bitcast_convert_fusion.1
  226.6 2.0 gather_fusion.2
  228.7 1.4 broadcast_select_fusion
  230.1 0.6 reshape.87
  230.7 2.1 multiply_reduce_fusion
  232.8 0.6 reshape.89
  233.4 2.1 reduce_sum.32
  (21 shorter events, 0.1 us)
Async XLA Ops:
  7.2 11.3 %copy-start = (bf16[128,1024]{1,0:T(8,128)(2,1)S(1)}, bf16[128,1024]{1,0:T(8,128)(2,1)}, u32[]{:S(2)}) copy-start(bf16[128,1024]{1,0:T(8,128)(2,1)} %param.11) | copy-start | bytes 786436
  85.2 51.5 %all-to-all-start = ((bf16[16,32,2048]{2,1,0:T(8,128)(2,1)}), bf16[16,32,2048]{2,1,0:T(8,128)(2,1)}, u32[]{:S(2)}, u32[]{:S(2)}) async-start(bf16[16,32,2048]{2,1,0:T(8,128)(2,1)} %bitcast.3), calls=%async_computation | async-start | bytes 4194304 | tf_op jit(solution)/shard_map/all_to_all | solution.py:14
  90.1 72.7 %reduce-scatter.5.cloned.1.call-start = ((), (), s32[]{:S(2)}) async-start(), calls=%async_computation.7 | async-start | bytes 3145728 | tf_op jit(solution)/shard_map/reduce_scatter | solution.py:25
  136.6 5.3 %copy-start.1 = (bf16[1,2048,1024]{2,1,0:T(8,128)(2,1)S(1)}, bf16[1,2048,1024]{2,1,0:T(8,128)(2,1)}, u32[]{:S(2)}) copy-start(bf16[1,2048,1024]{2,1,0:T(8,128)(2,1)} %param.15) | copy-start | bytes 12582916
  142.0 4.3 %copy-start.3 = (f32[512,1024]{1,0:T(8,128)S(1)}, f32[512,1024]{1,0:T(8,128)}, u32[]{:S(2)}) copy-start(f32[512,1024]{1,0:T(8,128)} %fusion) | copy-start | bytes 6291460
  146.2 6.9 %copy-start.4 = (bf16[512,1024]{1,0:T(8,128)(2,1)}, bf16[512,1024]{1,0:T(8,128)(2,1)S(1)}, u32[]{:S(2)}) copy-start(bf16[512,1024]{1,0:T(8,128)(2,1)S(1)} %get-tuple-element.14) | copy-start | bytes 3145732
  146.3 2.6 %copy-start.2 = (bf16[1,2048,1024]{2,1,0:T(8,128)(2,1)S(1)}, bf16[1,2048,1024]{2,1,0:T(8,128)(2,1)}, u32[]{:S(2)}) copy-start(bf16[1,2048,1024]{2,1,0:T(8,128)(2,1)} %param.14) | copy-start | bytes 12582916
  153.1 22.9 %reduce-scatter.3.cloned.1.call-start = ((), (), s32[]{:S(2)}) async-start(), calls=%async_computation.6 | async-start | bytes 3145728 | tf_op jit(solution)/shard_map/reduce_scatter | solution.py:25
  162.8 32.7 %all-to-all-start.3 = ((bf16[16,32,1024]{2,1,0:T(8,128)(2,1)}), bf16[16,32,1024]{2,1,0:T(8,128)(2,1)S(1)}, u32[]{:S(2)}, u32[]{:S(2)}) async-start(bf16[16,32,1024]{2,1,0:T(8,128)(2,1)} %bitcast.66), calls=%async_computation.5 | async-start | bytes 2097152 | tf_op jit(solution)/shard_map/all_to_all | solution.py:28
  195.5 29.6 %all-to-all-start.1 = ((bf16[16,32,1024]{2,1,0:T(8,128)(2,1)}), bf16[16,32,1024]{2,1,0:T(8,128)(2,1)}, u32[]{:S(2)}, u32[]{:S(2)}) async-start(bf16[16,32,1024]{2,1,0:T(8,128)(2,1)} %bitcast.65), calls=%async_computation.2 | async-start | bytes 2097152 | tf_op jit(solution)/shard_map/all_to_all | solution.py:28
Sparse Core Ops, SparseCore 0:
  153.2 9.5 reduce-scatter.4
  165.1 10.8 reduce-scatter.2
where the time goes:
time: 243 us; the launch traced here: 242 us
  waiting for transfers between devices  87.6 us (36%)
  blocking collectives  60.1 us (25%)
  matrix products  33.5 us (14%)
  local copies, waits for them, and re-layouts  17.6 us (7%)
  starting transfers between devices  17.2 us (7%)
  between operations  14.3 us (6%)
  other arithmetic  12.1 us (5%)
    all_to_all x1, blocking collectives, arrive(): lax.all_to_all(pick_rows(whole_rows, source_row, row_scale), 'expert', sp...  55.5 us
    all_to_all x1, waiting for transfers between devices, arrive(): lax.all_to_all(pick_rows(whole_rows, source_row, row_scale), 'expert', sp...  40.5 us
    all_to_all x2, waiting for transfers between devices, depart(): lax.all_to_all(shares.astype(jnp.bfloat16), 'expert', split_axis=0, conca...  37.1 us
    all_to_all x2, starting transfers between devices, depart(): lax.all_to_all(shares.astype(jnp.bfloat16), 'expert', split_axis=0, conca...  12 us
    reduce_scatter x2, waiting for transfers between devices, depart(): lax.psum_scatter(partial_sum.astype(jnp.bfloat16), 'mp', scatter_dimensio...  9.99 us
    dot_general x1, matrix products, shards(): jnp.dot(hidden, w_down_local, preferred_element_type=jnp.float32)  5.88 us
    dot_general x1, matrix products, shards(): lax.dot_general(arrived_grads, w_down_local, (((1,), (1,)), ((), ())), pr...  5.85 us
    gather x2, local copies, waits for them, and re-layouts, pick_rows(): picked_rows = jnp.take(source, source_row, axis=0)  5.74 us
  transfers between devices with their start and end apart: 5, of which 5 were waited for; matrix products, arithmetic and copies ran while one was open for 8% of the time, Pallas kernels for 0%

commit v1 on v0

v1 whole, which is shorter than its diff:
```python
import functools

import jax
import jax.numpy as jnp
from jax import lax
from jax.experimental import pallas as pl
from jax.experimental.pallas import tpu as pltpu
from jax.sharding import PartitionSpec as P

F32 = jnp.float32
BF16 = jnp.bfloat16


def ranks(ids, experts):
    top, rows = ids.shape
    names = lax.broadcasted_iota(jnp.int32, (experts, rows), 0)
    named = names == ids[0:1, :]
    for k in range(1, top):
        named = named | (names == ids[k : k + 1, :])
    before = lax.broadcasted_iota(jnp.int32, (rows, rows), 0) < lax.broadcasted_iota(
        jnp.int32, (rows, rows), 1
    )
    rank = jnp.dot(
        named.astype(F32).astype(BF16), before.astype(F32).astype(BF16), preferred_element_type=F32
    )
    return names, named, rank


def route_kernel(ids_ref, weight_ref, rows_ref, grads_ref, out_rows_ref, out_grads_ref, *, most):
    ids = ids_ref[...]
    weight = weight_ref[...]
    top, rows = ids.shape
    slots = out_rows_ref.shape[0]
    experts = slots // most
    names, named, rank = ranks(ids, experts)
    place = jnp.where(named, rank, -1.0)
    scale = jnp.zeros((experts, rows), F32)
    for k in range(top):
        scale = scale + jnp.where(names == ids[k : k + 1, :], weight[k : k + 1, :], 0.0)
    want = lax.broadcasted_iota(jnp.int32, (experts, most, rows), 1).astype(F32)
    hit = want == place[:, None, :]
    select = jnp.where(hit, 1.0, 0.0).reshape(slots, rows)
    scaled = jnp.where(hit, jnp.broadcast_to(scale[:, None, :], hit.shape), 0.0).reshape(slots, rows)
    scale_column = jnp.sum(scaled, axis=1, keepdims=True)
    select = select.astype(BF16)
    out_rows_ref[...] = jnp.dot(select, rows_ref[...], preferred_element_type=F32).astype(BF16)
    picked = jnp.dot(select, grads_ref[...], preferred_element_type=F32)
    out_grads_ref[...] = (picked * scale_column).astype(BF16)


def route(ids, weight, rows, grads, slots, most):
    width = rows.shape[1]
    shape = jax.ShapeDtypeStruct((slots, width), BF16)
    return pl.pallas_call(
        functools.partial(route_kernel, most=most),
        out_shape=(shape, shape),
        name="route",
    )(ids, weight, rows, grads)


def home_kernel(ids_ref, weight_ref, back_ref, out_ref, *, most, weighted):
    ids = ids_ref[...]
    top, rows = ids.shape
    slots = back_ref.shape[0]
    experts = slots // most
    names, named, rank = ranks(ids, experts)
    want = lax.broadcasted_iota(jnp.int32, (experts, most, rows), 1).astype(F32)
    back = back_ref[...]
    columns = jnp.transpose(weight_ref[...]) if weighted else None
    total = None
    for k in range(top):
        place = jnp.where(names == ids[k : k + 1, :], rank, -1.0)
        select = jnp.where(want == place[:, None, :], 1.0, 0.0).reshape(slots, rows).astype(BF16)
        part = lax.dot_general(select, back, (((0,), (0,)), ((), ())), preferred_element_type=F32)
        if weighted:
            part = part * columns[:, k : k + 1]
        total = part if total is None else total + part
    out_ref[...] = total.astype(BF16)


def home(ids, weight, back, most, weighted):
    return pl.pallas_call(
        functools.partial(home_kernel, most=most, weighted=weighted),
        out_shape=jax.ShapeDtypeStruct((ids.shape[1], back.shape[1]), BF16),
        name="home",
    )(ids, weight, back)


def across(rows):
    experts = lax.axis_size("expert")
    slots, width = rows.shape
    return lax.all_to_all(
        rows.reshape(experts, slots // experts, width), "expert", split_axis=0, concat_axis=0, tiled=True
    ).reshape(slots, width)


def whole_rows(half):
    parts_count = lax.axis_size("mp")
    width = half.shape[1]
    parts = [half]
    for k in range(1, parts_count):
        parts.append(
            lax.ppermute(half, "mp", [((j + k) % parts_count, j) for j in range(parts_count)])
        )
    both = jnp.concatenate(parts + parts[:-1], axis=1)
    first = (parts_count - lax.axis_index("mp")) % parts_count
    return lax.dynamic_slice_in_dim(both, first * width, parts_count * width, axis=1)


def share(partial):
    parts_count = lax.axis_size("mp")
    me = lax.axis_index("mp")
    width = partial.shape[1] // parts_count
    partial = partial.astype(BF16)
    total = lax.dynamic_slice_in_dim(partial, me * width, width, axis=1).astype(F32)
    for k in range(1, parts_count):
        other = lax.dynamic_slice_in_dim(partial, ((me + k) % parts_count) * width, width, axis=1)
        got = lax.ppermute(other, "mp", [(j, (j + k) % parts_count) for j in range(parts_count)])
        total = total + got.astype(F32)
    return total.astype(BF16)


def shards(tokens, expert_ids, combine, w_gate, w_up, w_down, grad_out):
    row_count = tokens.shape[0]
    expert_count = lax.axis_size("expert")
    most = 4 * row_count // expert_count
    slots = expert_count * most
    w_gate, w_up, w_down = w_gate[0], w_up[0], w_down[0]
    ids, weight = expert_ids.T, combine.T
    row_slots, grad_slots = route(ids, weight, tokens, grad_out, slots, most)
    rows = across(row_slots)
    rows, grad_slots = lax.optimization_barrier((rows, grad_slots))
    grads = across(grad_slots)
    rows = whole_rows(rows)
    gate = jnp.dot(rows, w_gate, preferred_element_type=F32)
    up = jnp.dot(rows, w_up, preferred_element_type=F32)
    sig = jax.nn.sigmoid(gate)
    hidden = (gate * sig * up).astype(BF16)
    out_partial = jnp.dot(hidden, w_down, preferred_element_type=F32)
    out_share = share(out_partial)
    out_back = across(out_share)
    output = home(ids, weight, out_back, most, True)
    grads = whole_rows(grads)
    grad_hidden = lax.dot_general(grads, w_down, (((1,), (1,)), ((), ())), preferred_element_type=F32)
    down_grad = lax.dot_general(hidden, grads, (((0,), (0,)), ((), ())), preferred_element_type=F32)
    grad_up = (grad_hidden * gate * sig).astype(BF16)
    grad_gate = (grad_hidden * up * sig * (1.0 + gate * (1.0 - sig))).astype(BF16)
    terms = lax.dot_general(grad_gate, w_gate, (((1,), (1,)), ((), ())), preferred_element_type=F32)
    terms = terms + lax.dot_general(grad_up, w_up, (((1,), (1,)), ((), ())), preferred_element_type=F32)
    grad_back = across(share(terms))
    grad_tokens = home(ids, weight, grad_back, most, False)
    return output, grad_tokens, down_grad.astype(BF16)[None]


def solution(mesh):
    return jax.shard_map(
        shards,
        mesh=mesh,
        in_specs=(
            P("expert", "mp"),
            P("expert", None),
            P("expert", None),
            P("expert", None, "mp"),
            P("expert", None, "mp"),
            P("expert", "mp", None),
            P("expert", "mp"),
        ),
        out_specs=(P("expert", "mp"), P("expert", "mp"), P("expert", "mp", None)),
        check_vma=False,
    )
```

time: 243 us -> 136 us (0.56)
  waiting for transfers between devices: 87.6 us -> 43.7 us
  blocking collectives: 60.1 us -> 32.9 us
  between operations: 14.3 us -> 0.82 us
  local copies, waits for them, and re-layouts: 17.6 us -> 5.44 us
  matrix products: 33.5 us -> 22 us
  Pallas kernels: 0 us -> 8.15 us
  other arithmetic: 12.1 us -> 7.18 us
    all_to_all x3, waiting for transfers between devices: 77.6 us -> 41 us  [across(): lax.all_to_all(rows.reshape(experts, slots // experts, width), 'expert',...]
    all_to_all x1, blocking collectives: 55.5 us -> 32.9 us  [across(): lax.all_to_all(rows.reshape(experts, slots // experts, width), 'expert',...]
    gather x5 -> x0, local copies, waits for them, and re-layouts: 12.4 us -> none  [the longest x2 5.74 us: pick_rows(): picked_rows = jnp.take(source, source_row, axis=0)]
    dot_general x7, matrix products: 33.5 us -> 22 us  [the longest x1 5.99 us: shards(): lax.dot_general(hidden, grads, (((0,), (0,)), ((), ())), preferred_elemen...]
    reduce_scatter x2 -> x0, waiting for transfers between devices: 9.99 us -> none  [depart(): lax.psum_scatter(partial_sum.astype(jnp.bfloat16), 'mp', scatter_dimensio...]
    pallas_call x0 -> x3, Pallas kernels: none -> 8.15 us  [the longest x2 5.2 us: home(): pl.pallas_call(functools.partial(home_kernel, most=most, weighted=weighte...]
    all_gather x2 -> x0, blocking collectives: 4.57 us -> none  [arrive(): whole_rows = lax.all_gather(local_rows, 'mp', axis=1, tiled=True)]
    reduce_sum x3 -> x0, other arithmetic: 4.23 us -> none  [the longest x2 4.14 us: depart(): combined = jnp.sum(gathered * pick_weight[:, :, None], axis=1)]
  transfers between devices with their start and end apart: 5 -> 7, of which waited for: 5 -> 4; matrix products, arithmetic and copies ran while one was open for 8% -> 22% of each run, Pallas kernels for 0% -> 2%
where the time goes in v1:
time: 136 us
  waiting for transfers between devices  43.7 us (32%)
  blocking collectives  32.9 us (24%)
  matrix products  22 us (16%)
  starting transfers between devices  15.4 us (11%)
  Pallas kernels  8.15 us (6%)
  other arithmetic  7.18 us (5%)
  local copies, waits for them, and re-layouts  5.44 us (4%)
    all_to_all x3, waiting for transfers between devices, across(): lax.all_to_all(rows.reshape(experts, slots // experts, width), 'expert',...  41 us
    all_to_all x1, blocking collectives, across(): lax.all_to_all(rows.reshape(experts, slots // experts, width), 'expert',...  32.9 us
    all_to_all x3, starting transfers between devices, across(): lax.all_to_all(rows.reshape(experts, slots // experts, width), 'expert',...  15.3 us
    dot_general x1, matrix products, shards(): lax.dot_general(hidden, grads, (((0,), (0,)), ((), ())), preferred_elemen...  5.99 us
    unnamed x30, local copies, waits for them, and re-layouts  5.24 us
    pallas_call x2, Pallas kernels, home(): pl.pallas_call(functools.partial(home_kernel, most=most, weighted=weighte...  5.2 us
    convert_element_type x2, other arithmetic, share(): return total.astype(BF16)  4.34 us
    dot_general x1, matrix products, shards(): up = jnp.dot(rows, w_up, preferred_element_type=F32)  3.74 us
  transfers between devices with their start and end apart: 7, of which 4 were waited for; matrix products, arithmetic and copies ran while one was open for 22% of the time, Pallas kernels for 2%

profile of v1, /device:TPU:8, one launch (start us, length us, event | category | flops | bytes accessed | tf_op | source)
XLA Modules:
  0.0 135.7 jit_solution(1588558137152557760)
XLA Ops:
  0.6 2.9 %route.1 = (bf16[512,1024]{1,0:T(8,128)(2,1)}, bf16[512,1024]{1,0:T(8,128)(2,1)}) custom-call(s32[2,128]{1,0:T(2,128)} %bitcast.47, f32[2,128]{1,0:T(2,128)} %bitcast.50, bf16[128,1024]{1,0:T(8,128)(2,1)} %rows_ref.1, bf16[128,1024]{1,0:T(8,128)(2,1)} %grads_ref.1), custom_call_target="tpu_custom_call" | custom-call | tf_op jit(solution)/shard_map/route/pallas_call | solution.py:54
  3.6 32.9 %all_to_all.20 = bf16[16,32,1024]{2,1,0:T(8,128)(2,1)S(1)} all-to-all(bf16[16,32,1024]{2,1,0:T(8,128)(2,1)} %bitcast.46), channel_id=1, replica_groups=mesh['expert'=16,'mp'=2] {'expert'}, dimensions={0} | all-to-all | bytes 2097152 | tf_op jit(solution)/shard_map/all_to_all | solution.py:92
  36.5 0.0 collective-permute-start
  36.5 4.6 %all-to-all-start.2 = ((bf16[16,32,1024]{2,1,0:T(8,128)(2,1)}), bf16[16,32,1024]{2,1,0:T(8,128)(2,1)S(1)}, u32[]{:S(2)}, u32[]{:S(2)}) async-start(bf16[16,32,1024]{2,1,0:T(8,128)(2,1)} %bitcast.45), calls=%async_computation.2 | async-start | bytes 2097152 | tf_op jit(solution)/shard_map/all_to_all | solution.py:92
  41.1 0.0 collective-permute-done
  41.1 1.4 %fusion.20 = bf16[512,2048]{1,0:T(8,128)(2,1)S(1)} fusion(s32[]{:T(128)S(6)} %select_n.28, bf16[512,1024]{1,0:T(8,128)(2,1)S(1)} %bitcast.40, bf16[512,1024]{1,0:T(8,128)(2,1)S(1)} %collective-permute-done), kind=kLoop, calls=%fused_computation.24 | loop fusion | flops 6291456 | bytes 4194308 | tf_op jit(solution)/shard_map/concatenate | solution.py:105
  42.5 0.7 copy-done.8
  43.3 2.3 %fusion.10 = f32[512,1024]{1,0:T(8,128)S(1)} fusion(bf16[512,2048]{1,0:T(8,128)(2,1)S(1)} %fusion.20, bf16[1,2048,1024]{2,1,0:T(8,128)(2,1)S(1)} %copy-done.8), kind=kOutput, calls=%fused_computation.10 | convolution fusion | flops 2147483648 | bytes 8388608 | tf_op jit(solution)/shard_map/dot_general | solution.py:135
  45.6 0.0 copy-done.6
  45.6 0.0 copy-start.10
  45.6 0.0 copy-start.4
  45.6 3.7 %multiply_convert_fusion.2 = (bf16[512,1024]{1,0:T(8,128)(2,1)S(1)}, f32[512,1024]{1,0:T(8,128)}) fusion(f32[512,1024]{1,0:T(8,128)S(1)} %fusion.10, bf16[512,2048]{1,0:T(8,128)(2,1)S(1)} %fusion.20, bf16[1,2048,1024]{2,1,0:T(8,128)(2,1)S(1)} %copy-done.6), kind=kOutput, calls=%fused_computation.29 | convolution fusion | flops 2150629376 | bytes 11534336 | tf_op jit(solution)/shard_map/dot_general | solution.py:136
  49.4 0.0 copy-done.10
  49.4 0.0 copy-done.4
  49.4 2.4 %fusion.14 = bf16[512,2048]{1,0:T(8,128)(2,1)S(1)} fusion(bf16[512,1024]{1,0:T(8,128)(2,1)S(1)} %get-tuple-element.11, bf16[1,1024,2048]{2,1,0:T(8,128)(2,1)S(1)} %copy-done.4), kind=kOutput, calls=%fused_computation.20 | convolution fusion | flops 2148532224 | bytes 7340032 | tf_op jit(solution)/shard_map/dot_general | solution.py:139
  51.7 0.0 copy-done.13
  51.7 0.0 copy-start.2
  51.7 0.1 constant_dynamic-slice_fusion.1
  51.8 1.2 copy-done.2
  53.0 0.0 collective-permute-start.1
  53.0 14.3 %all-to-all-done.2 = bf16[16,32,1024]{2,1,0:T(8,128)(2,1)S(1)} async-done(((bf16[16,32,1024]{2,1,0:T(8,128)(2,1)}), bf16[16,32,1024]{2,1,0:T(8,128)(2,1)S(1)}, u32[]{:S(2)}, u32[]{:S(2)}) %all-to-all-start.2) | async-done | bytes 1048608 | tf_op jit(solution)/shard_map/all_to_all | solution.py:92
  67.3 0.0 collective-permute-start.2
  67.3 0.0 collective-permute-done.1
  67.3 2.9 %add_convert_fusion.2 = bf16[512,1024]{1,0:T(8,128)(2,1)} fusion(bf16[512,1024]{1,0:T(8,128)(2,1)} %collective-permute-done.1, bf16[512,2048]{1,0:T(8,128)(2,1)} %copy-done.2, s32[]{:T(128)S(6)} %select_n.29), kind=kLoop, calls=%fused_computation.28 | loop fusion | flops 2097152 | bytes 3145732 | tf_op jit(solution)/shard_map/convert_element_type | solution.py:120
  70.2 5.4 %all-to-all-start.1 = ((bf16[16,32,1024]{2,1,0:T(8,128)(2,1)}), bf16[16,32,1024]{2,1,0:T(8,128)(2,1)S(1)}, u32[]{:S(2)}, u32[]{:S(2)}) async-start(bf16[16,32,1024]{2,1,0:T(8,128)(2,1)} %bitcast.7), calls=%async_computation.1 | async-start | bytes 2097152 | tf_op jit(solution)/shard_map/all_to_all | solution.py:92
  75.6 0.0 collective-permute-done.2
  75.7 1.4 %fusion.18 = bf16[512,2048]{1,0:T(8,128)(2,1)S(1)} fusion(s32[]{:T(128)S(6)} %select_n.28, bf16[512,1024]{1,0:T(8,128)(2,1)S(1)} %bitcast.42, bf16[512,1024]{1,0:T(8,128)(2,1)S(1)} %collective-permute-done.2), kind=kLoop, calls=%fused_computation.22 | loop fusion | flops 6291456 | bytes 4194308 | tf_op jit(solution)/shard_map/concatenate | solution.py:105
  77.1 0.0 copy-start.3
  77.1 1.3 copy-done.3
  78.4 0.0 copy-done.5
  78.4 2.4 %fusion = f32[512,1024]{1,0:T(8,128)S(1)} fusion(bf16[512,2048]{1,0:T(8,128)(2,1)S(1)} %fusion.18, bf16[1,1024,2048]{2,1,0:T(8,128)(2,1)S(1)} %copy-done.5), kind=kOutput, calls=%fused_computation | convolution fusion | flops 2147483648 | bytes 8388608 | tf_op jit(solution)/shard_map/dot_general | solution.py:144
  80.8 0.0 copy-done.7
  80.8 0.5 copy-done.11
  81.3 2.4 %fusion.4 = f32[512,2048]{1,0:T(8,128)S(1)} fusion(bf16[1,2048,1024]{2,1,0:T(8,128)(2,1)S(1)} %copy-done.7, f32[512,1024]{1,0:T(8,128)S(1)} %fusion, f32[512,1024]{1,0:T(8,128)S(1)} %copy-done.11), kind=kOutput, calls=%fused_computation.4 | convolution fusion | flops 2150629376 | bytes 12582912 | tf_op jit(solution)/shard_map/dot_general | solution.py:149
  83.6 0.5 copy-done.12
  84.1 2.9 %add_convert_fusion = bf16[512,2048]{1,0:T(8,128)(2,1)S(1)} fusion(f32[512,2048]{1,0:T(8,128)S(1)} %fusion.4, bf16[1,2048,1024]{2,1,0:T(8,128)(2,1)S(1)} %copy-done.9, f32[512,1024]{1,0:T(8,128)S(1)} %copy-done.11, f32[512,1024]{1,0:T(8,128)S(1)} %fusion, f32[512,1024]{1,0:T(8,128)S(1)} %copy-done.12), kind=kOutput, calls=%fused_computation.13 | convolution fusion | flops 2154823680 | bytes 16777216 | tf_op jit(solution)/shard_map/dot_general | solution.py:148
  87.0 0.1 constant_dynamic-slice_fusion
  87.1 0.1 collective-permute-start.3
  87.2 2.6 %collective-permute-done.3 = bf16[512,1024]{1,0:T(8,128)(2,1)S(1)} collective-permute-done((bf16[512,1024]{1,0:T(8,128)(2,1)S(1)}, bf16[512,1024]{1,0:T(8,128)(2,1)S(1)}, u32[]{:S(2)}, u32[]{:S(2)}) %collective-permute-start.3) | collective-permute-done | bytes 1048608 | tf_op jit(solution)/shard_map/ppermute | solution.py:118
  89.9 1.4 %add_convert_fusion.1 = bf16[512,1024]{1,0:T(8,128)(2,1)} fusion(bf16[512,1024]{1,0:T(8,128)(2,1)S(1)} %collective-permute-done.3, bf16[512,2048]{1,0:T(8,128)(2,1)S(1)} %add_convert_fusion, s32[]{:T(128)S(6)} %select_n.29), kind=kLoop, calls=%fused_computation.25 | loop fusion | flops 2097152 | bytes 3145732 | tf_op jit(solution)/shard_map/convert_element_type | solution.py:120
  91.3 10.6 %all-to-all-done.1 = bf16[16,32,1024]{2,1,0:T(8,128)(2,1)S(1)} async-done(((bf16[16,32,1024]{2,1,0:T(8,128)(2,1)}), bf16[16,32,1024]{2,1,0:T(8,128)(2,1)S(1)}, u32[]{:S(2)}, u32[]{:S(2)}) %all-to-all-start.1) | async-done | bytes 1048608 | tf_op jit(solution)/shard_map/all_to_all | solution.py:92
  101.9 5.4 %all-to-all-start.3 = ((bf16[16,32,1024]{2,1,0:T(8,128)(2,1)}), bf16[16,32,1024]{2,1,0:T(8,128)(2,1)S(1)}, u32[]{:S(2)}, u32[]{:S(2)}) async-start(bf16[16,32,1024]{2,1,0:T(8,128)(2,1)} %bitcast.11), calls=%async_computation.3 | async-start | bytes 2097152 | tf_op jit(solution)/shard_map/all_to_all | solution.py:92
  107.3 6.0 %convert_bitcast_fusion = bf16[1,1024,2048]{2,1,0:T(8,128)(2,1)} fusion(bf16[512,1024]{1,0:T(8,128)(2,1)S(1)} %copy-done.14, bf16[512,2048]{1,0:T(8,128)(2,1)} %copy-done.3), kind=kOutput, calls=%fused_computation.12 | convolution fusion | flops 2149580800 | bytes 7340032 | tf_op jit(solution)/shard_map/dot_general | solution.py:145
  113.3 0.0 copy-done
  113.3 2.6 %home.2 = bf16[128,1024]{1,0:T(8,128)(2,1)} custom-call(s32[2,128]{1,0:T(2,128)} %bitcast.48, f32[2,128]{1,0:T(2,128)} %bitcast.51, bf16[512,1024]{1,0:T(8,128)(2,1)} %bitcast.43), custom_call_target="tpu_custom_call" | custom-call | tf_op jit(solution)/shard_map/home/pallas_call | solution.py:82
  115.9 16.2 %all-to-all-done.3 = bf16[16,32,1024]{2,1,0:T(8,128)(2,1)S(1)} async-done(((bf16[16,32,1024]{2,1,0:T(8,128)(2,1)}), bf16[16,32,1024]{2,1,0:T(8,128)(2,1)S(1)}, u32[]{:S(2)}, u32[]{:S(2)}) %all-to-all-start.3) | async-done | bytes 1048608 | tf_op jit(solution)/shard_map/all_to_all | solution.py:92
  132.1 1.0 copy-done.1
  133.1 2.6 %home.3 = bf16[128,1024]{1,0:T(8,128)(2,1)} custom-call(s32[2,128]{1,0:T(2,128)} %bitcast.49, f32[2,128]{1,0:T(2,128)} %bitcast.52, bf16[512,1024]{1,0:T(8,128)(2,1)} %bitcast.44), custom_call_target="tpu_custom_call" | custom-call | tf_op jit(solution)/shard_map/home/pallas_call | solution.py:82
  (13 shorter events, 0.0 us)
Async XLA Ops:
  36.5 4.6 %collective-permute-start = (bf16[512,1024]{1,0:T(8,128)(2,1)S(1)}, bf16[512,1024]{1,0:T(8,128)(2,1)S(1)}, u32[]{:S(2)}, u32[]{:S(2)}) collective-permute-start(bf16[512,1024]{1,0:T(8,128)(2,1)S(1)} %bitcast.39), channel_id=1, source_target_pairs={{1,0},{0,1},{3,2},{2,3},{5,4},{4,5},{7,6},{6,7},{9,8},{8,9},{11,10... | collective-permute-start | bytes 3145736 | tf_op jit(solution)/shard_map/ppermute | solution.py:103
  36.5 30.8 %all-to-all-start.2 = ((bf16[16,32,1024]{2,1,0:T(8,128)(2,1)}), bf16[16,32,1024]{2,1,0:T(8,128)(2,1)S(1)}, u32[]{:S(2)}, u32[]{:S(2)}) async-start(bf16[16,32,1024]{2,1,0:T(8,128)(2,1)} %bitcast.45), calls=%async_computation.2 | async-start | bytes 2097152 | tf_op jit(solution)/shard_map/all_to_all | solution.py:92
  41.1 2.2 %copy-start.8 = (bf16[1,2048,1024]{2,1,0:T(8,128)(2,1)S(1)}, bf16[1,2048,1024]{2,1,0:T(8,128)(2,1)}, u32[]{:S(2)}) copy-start(bf16[1,2048,1024]{2,1,0:T(8,128)(2,1)} %param.10) | copy-start | bytes 12582916
  43.3 2.3 %copy-start.6 = (bf16[1,2048,1024]{2,1,0:T(8,128)(2,1)S(1)}, bf16[1,2048,1024]{2,1,0:T(8,128)(2,1)}, u32[]{:S(2)}) copy-start(bf16[1,2048,1024]{2,1,0:T(8,128)(2,1)} %param.11) | copy-start | bytes 12582916
  45.6 3.8 %copy-start.10 = (f32[512,1024]{1,0:T(8,128)}, f32[512,1024]{1,0:T(8,128)S(1)}, u32[]{:S(2)}) copy-start(f32[512,1024]{1,0:T(8,128)S(1)} %fusion.10) | copy-start | bytes 6291460
  45.6 3.8 %copy-start.4 = (bf16[1,1024,2048]{2,1,0:T(8,128)(2,1)S(1)}, bf16[1,1024,2048]{2,1,0:T(8,128)(2,1)}, u32[]{:S(2)}) copy-start(bf16[1,1024,2048]{2,1,0:T(8,128)(2,1)} %param.12) | copy-start | bytes 12582916
  49.4 2.4 %copy-start.13 = (bf16[512,1024]{1,0:T(8,128)(2,1)}, bf16[512,1024]{1,0:T(8,128)(2,1)S(1)}, u32[]{:S(2)}) copy-start(bf16[512,1024]{1,0:T(8,128)(2,1)S(1)} %get-tuple-element.11) | copy-start | bytes 3145732
  51.7 1.3 copy-start.2
  53.0 14.3 %collective-permute-start.1 = (bf16[512,1024]{1,0:T(8,128)(2,1)S(1)}, bf16[512,1024]{1,0:T(8,128)(2,1)}, u32[]{:S(2)}, u32[]{:S(2)}) collective-permute-start(bf16[512,1024]{1,0:T(8,128)(2,1)S(1)} %constant_dynamic-slice_fusion.1), channel_id=1, source_target_pairs={{0,1},{1,0},{2,3},{3,2},{4,5},{5,4},{6,7},{7,6},{8,9},{9,8},{10,11... | collective-permute-start | bytes 3145736 | tf_op jit(solution)/shard_map/ppermute | solution.py:118
  67.3 8.3 %collective-permute-start.2 = (bf16[512,1024]{1,0:T(8,128)(2,1)S(1)}, bf16[512,1024]{1,0:T(8,128)(2,1)S(1)}, u32[]{:S(2)}, u32[]{:S(2)}) collective-permute-start(bf16[512,1024]{1,0:T(8,128)(2,1)S(1)} %bitcast.41), channel_id=1, source_target_pairs={{1,0},{0,1},{3,2},{2,3},{5,4},{4,5},{7,6},{6,7},{9,8},{8,9},{11,10... | collective-permute-start | bytes 3145736 | tf_op jit(solution)/shard_map/ppermute | solution.py:103
  70.2 31.6 %all-to-all-start.1 = ((bf16[16,32,1024]{2,1,0:T(8,128)(2,1)}), bf16[16,32,1024]{2,1,0:T(8,128)(2,1)S(1)}, u32[]{:S(2)}, u32[]{:S(2)}) async-start(bf16[16,32,1024]{2,1,0:T(8,128)(2,1)} %bitcast.7), calls=%async_computation.1 | async-start | bytes 2097152 | tf_op jit(solution)/shard_map/all_to_all | solution.py:92
  75.6 2.7 %copy-start.5 = (bf16[1,1024,2048]{2,1,0:T(8,128)(2,1)S(1)}, bf16[1,1024,2048]{2,1,0:T(8,128)(2,1)}, u32[]{:S(2)}) copy-start(bf16[1,1024,2048]{2,1,0:T(8,128)(2,1)} %param.12) | copy-start | bytes 12582916
  77.1 1.3 copy-start.3
  78.4 2.4 %copy-start.7 = (bf16[1,2048,1024]{2,1,0:T(8,128)(2,1)S(1)}, bf16[1,2048,1024]{2,1,0:T(8,128)(2,1)}, u32[]{:S(2)}) copy-start(bf16[1,2048,1024]{2,1,0:T(8,128)(2,1)} %param.11) | copy-start | bytes 12582916
  78.4 2.9 %copy-start.11 = (f32[512,1024]{1,0:T(8,128)S(1)}, f32[512,1024]{1,0:T(8,128)}, u32[]{:S(2)}) copy-start(f32[512,1024]{1,0:T(8,128)} %copy-done.10) | copy-start | bytes 6291460
  81.2 2.4 %copy-start.9 = (bf16[1,2048,1024]{2,1,0:T(8,128)(2,1)S(1)}, bf16[1,2048,1024]{2,1,0:T(8,128)(2,1)}, u32[]{:S(2)}) copy-start(bf16[1,2048,1024]{2,1,0:T(8,128)(2,1)} %param.10) | copy-start | bytes 12582916
  81.3 2.9 %copy-start.12 = (f32[512,1024]{1,0:T(8,128)S(1)}, f32[512,1024]{1,0:T(8,128)}, u32[]{:S(2)}) copy-start(f32[512,1024]{1,0:T(8,128)} %get-tuple-element.12) | copy-start | bytes 6291460
  87.1 20.2 %copy-start.14 = (bf16[512,1024]{1,0:T(8,128)(2,1)S(1)}, bf16[512,1024]{1,0:T(8,128)(2,1)}, u32[]{:S(2)}) copy-start(bf16[512,1024]{1,0:T(8,128)(2,1)} %copy-done.13) | copy-start | bytes 3145732
  87.1 2.7 %collective-permute-start.3 = (bf16[512,1024]{1,0:T(8,128)(2,1)S(1)}, bf16[512,1024]{1,0:T(8,128)(2,1)S(1)}, u32[]{:S(2)}, u32[]{:S(2)}) collective-permute-start(bf16[512,1024]{1,0:T(8,128)(2,1)S(1)} %constant_dynamic-slice_fusion), channel_id=1, source_target_pairs={{0,1},{1,0},{2,3},{3,2},{4,5},{5,4},{6,7},{7,6},{8,9},{9,8},{10,11... | collective-permute-start | bytes 3145736 | tf_op jit(solution)/shard_map/ppermute | solution.py:118
  101.9 11.4 %copy-start = (bf16[16,32,1024]{2,1,0:T(8,128)(2,1)}, bf16[16,32,1024]{2,1,0:T(8,128)(2,1)S(1)}, u32[]{:S(2)}) copy-start(bf16[16,32,1024]{2,1,0:T(8,128)(2,1)S(1)} %all-to-all-done.1) | copy-start | bytes 3145732
  101.9 30.2 %all-to-all-start.3 = ((bf16[16,32,1024]{2,1,0:T(8,128)(2,1)}), bf16[16,32,1024]{2,1,0:T(8,128)(2,1)S(1)}, u32[]{:S(2)}, u32[]{:S(2)}) async-start(bf16[16,32,1024]{2,1,0:T(8,128)(2,1)} %bitcast.11), calls=%async_computation.3 | async-start | bytes 2097152 | tf_op jit(solution)/shard_map/all_to_all | solution.py:92
  132.1 1.0 copy-start.1

commit v2 on v0

v2 whole, which is shorter than its diff:
```python
import functools

import jax
import jax.numpy as jnp
from jax import lax
from jax.experimental import pallas as pl
from jax.experimental.pallas import tpu as pltpu
from jax.sharding import PartitionSpec as P


F32 = jnp.float32
BF16 = jnp.bfloat16
SMEM = pl.BlockSpec(memory_space=pltpu.SMEM)
VMEM = pl.BlockSpec(memory_space=pltpu.VMEM)


def cost(flops, nbytes):
    return pl.CostEstimate(flops=flops, bytes_accessed=nbytes, transcendentals=0)


def ranks(ids, first, experts):
    top, rows = ids.shape
    names = lax.broadcasted_iota(jnp.int32, (experts, rows), 0) + first
    named = names == ids[0:1, :]
    for k in range(1, top):
        named = named | (names == ids[k : k + 1, :])
    before = lax.broadcasted_iota(jnp.int32, (rows, rows), 0) < lax.broadcasted_iota(
        jnp.int32, (rows, rows), 1
    )
    rank = jnp.dot(
        jnp.where(named, 1.0, 0.0).astype(BF16),
        jnp.where(before, 1.0, 0.0).astype(BF16),
        preferred_element_type=F32,
    )
    return names, named, rank


def split_table(refs, top):
    if len(refs) == 2:
        return refs[0][...], refs[1][...]
    table = refs[0][...]
    return table[:top, :].astype(jnp.int32), table[top:, :]


def take(refs, counts):
    groups, at = [], 0
    for count in counts:
        groups.append(refs[at : at + count])
        at += count
    return groups, refs[at:]


def slots_kernel(first_ref, *refs, counts, most, top, scaled):
    groups, rest = take(refs, counts)
    out_ref = rest[-1]
    experts = out_ref.shape[0]
    first = first_ref[0]
    for s, group in enumerate(groups):
        ids, weight = split_table(group, top)
        rows = rest[s][...]
        count = rows.shape[0]
        names, named, rank = ranks(ids, first, experts)
        place = jnp.where(named, rank, -1.0)
        want = lax.broadcasted_iota(jnp.int32, (experts, most, count), 1).astype(F32)
        hit = want == place[:, None, :]
        select = jnp.where(hit, 1.0, 0.0).reshape(experts * most, count).astype(BF16)
        picked = jnp.dot(select, rows, preferred_element_type=F32)
        if scaled:
            scale = jnp.zeros((experts, count), F32)
            for k in range(top):
                scale = scale + jnp.where(names == ids[k : k + 1, :], weight[k : k + 1, :], 0.0)
            spread = jnp.where(hit, jnp.broadcast_to(scale[:, None, :], hit.shape), 0.0)
            picked = picked * jnp.sum(spread.reshape(experts * most, count), axis=1, keepdims=True)
        out_ref[:, s * most : (s + 1) * most, :] = picked.astype(BF16).reshape(experts, most, -1)


def build_slots(first, tables, rows, experts, most, top, scaled):
    flat = [t for table in tables for t in table]
    count, width = rows[0].shape
    return pl.pallas_call(
        functools.partial(
            slots_kernel, counts=[len(t) for t in tables], most=most, top=top, scaled=scaled
        ),
        in_specs=[SMEM] + [VMEM] * (len(flat) + len(rows)),
        out_specs=VMEM,
        out_shape=jax.ShapeDtypeStruct((experts, len(rows) * most, width), BF16),
        cost_estimate=cost(
            2 * len(rows) * experts * most * count * width, 2 * len(rows) * (count + experts * most) * width
        ),
        name="slots",
    )(first, *flat, *rows)


def home_kernel(first_ref, *refs, counts, at, most, top, weighted):
    groups, rest = take(refs, counts)
    back_ref = rest[0]
    outs = rest[1:]
    experts, _, width = back_ref.shape
    first = first_ref[0]
    for s, group in enumerate(groups):
        ids, weight = split_table(group, top)
        count = ids.shape[1]
        names, named, rank = ranks(ids, first, experts)
        want = lax.broadcasted_iota(jnp.int32, (experts, most, count), 1).astype(F32)
        back = back_ref[:, at[s] * most : (at[s] + 1) * most, :].reshape(experts * most, width)
        picks = [names == ids[k : k + 1, :] for k in range(top)] if weighted else [named]
        columns = jnp.transpose(weight) if weighted else None
        total = None
        for k, chosen in enumerate(picks):
            place = jnp.where(chosen, rank, -1.0)
            select = jnp.where(want == place[:, None, :], 1.0, 0.0)
            select = select.reshape(experts * most, count).astype(BF16)
            part = lax.dot_general(select, back, (((0,), (0,)), ((), ())), preferred_element_type=F32)
            if weighted:
                part = part * columns[:, k : k + 1]
            total = part if total is None else total + part
        outs[s][...] = total.astype(outs[s].dtype)


def bring_home(first, tables, back, at, kinds, count, most, top, weighted):
    flat = [t for table in tables for t in table]
    width = back.shape[2]
    return pl.pallas_call(
        functools.partial(
            home_kernel, counts=[len(t) for t in tables], at=at, most=most, top=top, weighted=weighted
        ),
        in_specs=[SMEM] + [VMEM] * (len(flat) + 1),
        out_specs=[VMEM] * len(tables),
        out_shape=[jax.ShapeDtypeStruct((count, width), kind) for kind in kinds],
        cost_estimate=cost(2 * back.size * count * (top if weighted else 1), 2 * back.size),
        name="home",
    )(first, *flat, back)


def blocks(hidden_width):
    return 256 if hidden_width % 256 == 0 else hidden_width


def spans(me_ref, parts, width):
    return [pl.ds(pl.multiple_of(lax.rem(me_ref[0] + k, parts) * width, width), width) for k in range(parts)]


NT = (((1,), (1,)), ((), ()))
TN = (((0,), (0,)), ((), ()))


def weight_kernel(me_ref, *refs, parts, width, chunks):
    gs, hiddens, out_ref = refs[:parts], refs[parts:-1], refs[-1]
    where = spans(me_ref, parts, width)
    experts, _, most, _ = gs[0].shape
    for k in range(parts):
        g = gs[k][...].reshape(experts * chunks * most, width)
        total = lax.dot_general(hiddens[0][...], g, TN, preferred_element_type=F32)
        out_ref[0, :, where[k]] = total.astype(BF16)


def weight_grad(me, gs, hiddens):
    parts, (experts, chunks, most, width) = len(gs), gs[0].shape
    rows, hid = hiddens[0].shape
    block = blocks(hid)
    whole = pl.BlockSpec((experts, chunks, most, width), lambda j: (0, 0, 0, 0))
    return pl.pallas_call(
        functools.partial(weight_kernel, parts=parts, width=width, chunks=chunks),
        grid=(hid // block,),
        in_specs=[SMEM] + [whole] * parts + [pl.BlockSpec((rows, block), lambda j: (0, j))],
        out_specs=pl.BlockSpec((1, block, parts * width), lambda j: (0, j, 0)),
        out_shape=jax.ShapeDtypeStruct((1, hid, parts * width), BF16),
        cost_estimate=cost(2 * chunks * rows * hid * parts * width, 2 * hid * parts * width),
        name="weight_grad",
    )(me, *gs, *hiddens)


def over(value):
    experts = lax.axis_size("expert")
    return lax.ppermute(value, "expert", [(j, (j + experts // 2) % experts) for j in range(experts)])


def within(slots):
    experts = lax.axis_size("expert")
    groups = [list(range(experts // 2)), list(range(experts // 2, experts))]
    return lax.all_to_all(
        slots, "expert", split_axis=0, concat_axis=0, tiled=True, axis_index_groups=groups
    )


def gather_parts(value):
    parts = lax.axis_size("mp")
    return [value] + [lax.ppermute(value, "mp", [((j + k) % parts, j) for j in range(parts)]) for k in range(1, parts)]


def give_parts(values):
    parts = lax.axis_size("mp")
    return [values[0]] + [
        lax.ppermute(values[k], "mp", [(j, (j + k) % parts) for j in range(parts)])
        for k in range(1, parts)
    ]


def added(values):
    total = values[0].astype(F32)
    for value in values[1:]:
        total = total + value.astype(F32)
    return total.astype(BF16)


def rank_slices(weight, axis):
    parts = lax.axis_size("mp")
    width = weight.shape[axis] // parts
    me = lax.axis_index("mp")
    return [
        lax.dynamic_slice_in_dim(weight, ((me + k) % parts) * width, width, axis=axis) for k in range(parts)
    ]


def dot(a, b, dims=(((1,), (0,)), ((), ()))):
    return lax.dot_general(a, b, dims, preferred_element_type=F32)


def joined(parts):
    count, width = len(parts), parts[0].shape[1]
    both = jnp.concatenate(parts + parts[:-1], axis=1)
    first = (count - lax.axis_index("mp")) % count
    return lax.dynamic_slice_in_dim(both, first * width, count * width, axis=1)


def body(tokens, expert_ids, combine, w_gate, w_up, w_down, grad_out):
    row_count, top = expert_ids.shape
    expert_count = lax.axis_size("expert")
    most = 4 * row_count // expert_count
    half = expert_count // 2
    width = tokens.shape[1]
    rows = 2 * half * most
    gates, ups, downs = rank_slices(w_gate[0], 0), rank_slices(w_up[0], 0), rank_slices(w_down[0], 1)
    first = ((lax.axis_index("expert") // half) * half).astype(jnp.int32).reshape(1)
    me = lax.axis_index("mp").astype(jnp.int32).reshape(1)
    near = (expert_ids.T, combine.T)
    far_tokens = over(tokens)
    far = (over(jnp.concatenate([near[0].astype(F32), near[1]], axis=0)),)
    far_grads = over(grad_out)
    t_slots = build_slots(first, (near, far), (tokens, far_tokens), half, most, top, False)
    t_rows = within(t_slots)
    grad_slots = build_slots(first, (near, far), (grad_out, far_grads), half, most, top, True)
    grads = within(grad_slots)
    xs = gather_parts(t_rows.reshape(rows, width))
    x = joined(xs)
    gate = dot(x, w_gate[0])
    up = dot(x, w_up[0])
    sig = jax.nn.sigmoid(gate)
    hidden = (gate * sig * up).astype(BF16)
    outs = [dot(hidden, w).astype(BF16) for w in reversed(downs)][::-1]
    outs[0] = lax.optimization_barrier(outs[0])
    out_given = give_parts(outs)
    out_slots = added(out_given)
    grads, out_slots = lax.optimization_barrier((grads, out_slots))
    out_back = within(out_slots.reshape(half, 2 * most, width))
    out_near, out_far = bring_home(
        first, (near, far), out_back, (0, 1), (F32, BF16), row_count, most, top, True
    )
    out_over = over(out_far)
    output = (out_near + out_over.astype(F32)).astype(BF16)
    gs = gather_parts(grads.reshape(rows, width))
    g = joined(gs)
    grad_hidden = dot(g, w_down[0], NT)
    grad_up = (grad_hidden * gate * sig).astype(BF16)
    grad_gate = (grad_hidden * up * sig * (1.0 + gate * (1.0 - sig))).astype(BF16)
    terms = []
    for k in reversed(range(len(gs))):
        terms.append((dot(grad_gate, gates[k], NT) + dot(grad_up, ups[k], NT)).astype(BF16))
    terms = terms[::-1]
    terms[0] = lax.optimization_barrier(terms[0])
    given = give_parts(terms)
    down_grad = weight_grad(me, [g.reshape(half, 2, most, width) for g in gs], (hidden,))
    grad_back = within(added(given).reshape(half, 2 * most, width))
    grad_near, grad_far = bring_home(first, (near, far), grad_back, (0, 1), (F32, BF16), row_count, most, top, False)
    grad_over = over(grad_far)
    grad_tokens = (grad_near + grad_over.astype(F32)).astype(BF16)
    return output, grad_tokens, down_grad


def solution(mesh):
    return jax.shard_map(
        body,
        mesh=mesh,
        in_specs=(
            P("expert", "mp"),
            P("expert", None),
            P("expert", None),
            P("expert", None, "mp"),
            P("expert", None, "mp"),
            P("expert", "mp", None),
            P("expert", "mp"),
        ),
        out_specs=(P("expert", "mp"), P("expert", "mp"), P("expert", "mp", None)),
        check_vma=False,
    )
```

time: 243 us -> 141 us (0.58)
  the two profiles are of different devices: /device:TPU:8 before, /device:TPU:0 now
where the time goes in v2:
time: 141 us; the launch traced here: 140 us
  waiting for transfers between devices  45.7 us (32%)
  matrix products  23.5 us (17%)
  starting transfers between devices  22.7 us (16%)
  blocking collectives  19.2 us (14%)
  Pallas kernels  17.3 us (12%)
  other arithmetic  7.09 us (5%)
  local copies, waits for them, and re-layouts  4.05 us (3%)
    ppermute x5, waiting for transfers between devices, over(): lax.ppermute(value, 'expert', [(j, (j + experts // 2) % experts) for j in...  29.7 us
    dot_general x9, matrix products, dot(): return lax.dot_general(a, b, dims, preferred_element_type=F32)  23.5 us
    all_to_all x1, blocking collectives, within(): lax.all_to_all(slots, 'expert', split_axis=0, concat_axis=0, tiled=True,...  19.2 us
    all_to_all x3, waiting for transfers between devices, within(): lax.all_to_all(slots, 'expert', split_axis=0, concat_axis=0, tiled=True,...  16 us
    all_to_all x3, starting transfers between devices, within(): lax.all_to_all(slots, 'expert', split_axis=0, concat_axis=0, tiled=True,...  13.3 us
    ppermute x5, starting transfers between devices, over(): lax.ppermute(value, 'expert', [(j, (j + experts // 2) % experts) for j in...  8.81 us
    pallas_call x1, Pallas kernels, weight_grad(): pl.pallas_call(functools.partial(weight_kernel, parts=parts, width=width,...  6.27 us
    pallas_call x2, Pallas kernels, bring_home(): pl.pallas_call(functools.partial(home_kernel, counts=[len(t) for t in tab...  5.59 us
  transfers between devices with their start and end apart: 12, of which 5 were waited for; matrix products, arithmetic and copies ran while one was open for 21% of the time, Pallas kernels for 10%

profile of v2, /device:TPU:0, one launch (start us, length us, event | category | flops | bytes accessed | tf_op | source)
XLA Modules:
  0.0 140.4 jit_solution(7179074149271094056)
XLA Ops:
  0.6 0.0 copy-start.5
  0.6 4.1 %collective-permute-start.2 = (bf16[128,1024]{1,0:T(8,128)(2,1)}, bf16[128,1024]{1,0:T(8,128)(2,1)S(1)}, u32[]{:S(2)}, u32[]{:S(2)}) collective-permute-start(bf16[128,1024]{1,0:T(8,128)(2,1)} %refs_3_.3), channel_id=1, source_target_pairs={{0,16},{2,18},{4,20},{6,22},{8,24},{10,26},{12,28},{14,30},{16,0},... | collective-permute-start | bytes 786440 | tf_op jit(solution)/shard_map/ppermute | solution.py:175
  4.8 0.7 bitcast_convert_fusion
  5.5 0.7 pad_maximum_fusion
  6.1 0.0 collective-permute-start
  6.2 10.8 %collective-permute-done.refs_2_ = f32[4,128]{1,0:T(4,128)S(1)} collective-permute-done((f32[4,128]{1,0:T(4,128)S(1)}, f32[4,128]{1,0:T(4,128)S(1)}, u32[]{:S(2)}, u32[]{:S(2)}) %collective-permute-start) | collective-permute-done | bytes 2080 | tf_op jit(solution)/shard_map/ppermute | solution.py:175
  17.0 0.6 copy-done.8
  17.6 0.1 copy-done.7
  17.7 2.7 %slots.3 = bf16[8,64,1024]{2,1,0:T(8,128)(2,1)} custom-call(s32[1]{0:T(128)} %bitcast.first_ref, s32[2,128]{1,0:T(2,128)} %bitcast.63, f32[2,128]{1,0:T(2,128)} %bitcast.68, f32[4,128]{1,0:T(4,128)} %copy-done.8, bf16[128,1024]{1,0:T(8,128)(2,1)} %refs_3_.3, bf16[128,1024]{1,0:T(8,128)(2,1)} %copy-done.7), custom_call_target="tpu_custom_call" | custom-call | flops 134217728 | bytes 1572864 | tf_op jit(solution)/shard_map/slots/pallas_call | solution.py:80
  20.4 19.2 %all_to_all.20 = bf16[8,64,1024]{2,1,0:T(8,128)(2,1)S(1)} all-to-all(bf16[8,64,1024]{2,1,0:T(8,128)(2,1)} %slots.3), channel_id=1, replica_groups={{0,2,4,6,8,10,12,14},{16,18,20,22,24,26,28,30},{1,3,5,7,9,11,13,15},{17..., dimensions={0} | all-to-all | bytes 2097152 | tf_op jit(solution)/shard_map/all_to_all | solution.py:181
  39.6 3.3 %collective-permute-start.1 = (bf16[128,1024]{1,0:T(8,128)(2,1)S(1)}, bf16[128,1024]{1,0:T(8,128)(2,1)S(1)}, u32[]{:S(2)}, u32[]{:S(2)}) collective-permute-start(bf16[128,1024]{1,0:T(8,128)(2,1)S(1)} %copy-done.5), channel_id=1, source_target_pairs={{0,16},{2,18},{4,20},{6,22},{8,24},{10,26},{12,28},{14,30},{16,0},... | collective-permute-start | bytes 786440 | tf_op jit(solution)/shard_map/ppermute | solution.py:175
  42.9 12.6 %collective-permute-done.1.refs_4_ = bf16[128,1024]{1,0:T(8,128)(2,1)S(1)} collective-permute-done((bf16[128,1024]{1,0:T(8,128)(2,1)S(1)}, bf16[128,1024]{1,0:T(8,128)(2,1)S(1)}, u32[]{:S(2)}, u32[]{:S(2)}) %collective-permute-start.1) | collective-permute-done | bytes 262176 | tf_op jit(solution)/shard_map/ppermute | solution.py:175
  55.5 0.7 copy-done.6
  56.2 2.7 %slots.2 = bf16[8,64,1024]{2,1,0:T(8,128)(2,1)} custom-call(s32[1]{0:T(128)} %bitcast.first_ref, s32[2,128]{1,0:T(2,128)} %bitcast.64, f32[2,128]{1,0:T(2,128)} %bitcast.69, f32[4,128]{1,0:T(4,128)} %copy-done.8, bf16[128,1024]{1,0:T(8,128)(2,1)} %refs_3_.2, bf16[128,1024]{1,0:T(8,128)(2,1)} %copy-done.6), custom_call_target="tpu_custom_call" | custom-call | flops 134217728 | bytes 1572864 | tf_op jit(solution)/shard_map/slots/pallas_call | solution.py:80
  58.9 3.6 %all-to-all-start = ((bf16[8,64,1024]{2,1,0:T(8,128)(2,1)}), bf16[8,64,1024]{2,1,0:T(8,128)(2,1)S(1)}, u32[]{:S(2)}, u32[]{:S(2)}) async-start(bf16[8,64,1024]{2,1,0:T(8,128)(2,1)} %slots.2), calls=%async_computation | async-start | bytes 2097152 | tf_op jit(solution)/shard_map/all_to_all | solution.py:181
  62.5 0.0 copy-start.12
  62.5 1.4 %fusion.10 = bf16[512,2048]{1,0:T(8,128)(2,1)S(1)} fusion(s32[]{:T(128)S(6)} %select_n.45, bf16[512,1024]{1,0:T(8,128)(2,1)S(1)} %bitcast.59, bf16[512,1024]{1,0:T(8,128)(2,1)S(1)} %collective-permute-done.3), kind=kLoop, calls=%fused_computation.15 | loop fusion | flops 6291456 | bytes 4194308 | tf_op jit(solution)/shard_map/concatenate | solution.py:221
  63.9 0.7 copy-done.12
  64.7 2.3 %fusion.4 = f32[512,1024]{1,0:T(8,128)S(1)} fusion(bf16[512,2048]{1,0:T(8,128)(2,1)S(1)} %fusion.10, bf16[1,2048,1024]{2,1,0:T(8,128)(2,1)S(1)} %copy-done.12), kind=kOutput, calls=%fused_computation.4 | convolution fusion | flops 2147483648 | bytes 8388608 | tf_op jit(solution)/shard_map/dot_general | solution.py:216
  67.0 0.0 copy-start.9
  67.1 3.7 %multiply_convert_fusion.2 = (bf16[512,1024]{1,0:T(8,128)(2,1)S(1)}, f32[512,1024]{1,0:T(8,128)}) fusion(f32[512,1024]{1,0:T(8,128)S(1)} %fusion.4, bf16[512,2048]{1,0:T(8,128)(2,1)S(1)} %fusion.10, bf16[1,2048,1024]{2,1,0:T(8,128)(2,1)S(1)} %copy-done.10), kind=kOutput, calls=%fused_computation.40 | convolution fusion | flops 2150629376 | bytes 11534336 | tf_op jit(solution)/shard_map/dot_general | solution.py:216
  70.8 2.3 %fusion.32 = bf16[512,1024]{1,0:T(8,128)(2,1)} fusion(bf16[512,1024]{1,0:T(8,128)(2,1)S(1)} %get-tuple-element.17.refs_2_, bf16[1,1024,2048]{2,1,0:T(8,128)(2,1)S(1)} %copy-done.9, s32[]{:T(128)S(6)} %select_n.49), kind=kOutput, calls=%fused_computation.43 | convolution fusion | flops 1074266112 | bytes 4194308 | tf_op jit(solution)/shard_map/dot_general | solution.py:216
  73.1 3.2 %fusion.29 = bf16[512,1024]{1,0:T(8,128)(2,1)S(1)} fusion(bf16[512,1024]{1,0:T(8,128)(2,1)} %copy-done.15, bf16[1,1024,2048]{2,1,0:T(8,128)(2,1)} %param.12, s32[]{:T(128)S(6)} %select_n.47), kind=kOutput, calls=%fused_computation.42 | convolution fusion | flops 1074266112 | bytes 4194308 | tf_op jit(solution)/shard_map/dot_general | solution.py:216
  76.3 1.4 add_convert_fusion.3
  77.7 0.5 collective-permute-start.6
  78.2 5.0 %all-to-all-start.2 = ((bf16[8,64,1024]{2,1,0:T(8,128)(2,1)}), bf16[8,64,1024]{2,1,0:T(8,128)(2,1)S(1)}, u32[]{:S(2)}, u32[]{:S(2)}) async-start(bf16[8,64,1024]{2,1,0:T(8,128)(2,1)} %bitcast.8), calls=%async_computation.2 | async-start | bytes 2097152 | tf_op jit(solution)/shard_map/all_to_all | solution.py:181
  83.2 0.0 copy-start.11
  83.2 6.8 %multiply_convert_fusion.1 = (bf16[512,1024]{1,0:T(8,128)(2,1)S(1)}, bf16[512,1024]{1,0:T(8,128)(2,1)S(1)}) fusion(f32[512,1024]{1,0:T(8,128)} %copy-done.16, f32[512,1024]{1,0:T(8,128)} %get-tuple-element.18, bf16[1,1024,2048]{2,1,0:T(8,128)(2,1)} %param.12, s32[]{:T(128)S(6)} %select_n.45, bf16[512,1024]{1,0:T(8,128)(2,1)S(1)} %bitcast.61, ...), kind=kOutput, calls=%fused_computation.36 | convolution fusion | flops 2160590848 | bytes 12582916 | tf_op jit(solution)/shard_map/dot_general | solution.py:216
  90.0 0.0 copy-start.13
  90.1 1.3 fusion.11
  91.4 0.9 copy-done.13
  92.2 1.3 add_convert_fusion.1
  93.5 0.1 collective-permute-start.7
  93.6 1.3 fusion.15
  94.9 1.3 add_convert_fusion.2
  96.2 0.0 collective-permute-done.7
  96.3 1.4 add_convert_fusion
  97.7 0.3 all-to-all-done.2.refs_3_
  98.0 4.8 %all-to-all-start.3 = ((bf16[8,64,1024]{2,1,0:T(8,128)(2,1)}), bf16[8,64,1024]{2,1,0:T(8,128)(2,1)S(1)}, u32[]{:S(2)}, u32[]{:S(2)}) async-start(bf16[8,64,1024]{2,1,0:T(8,128)(2,1)} %bitcast.15), calls=%async_computation.3 | async-start | bytes 2097152 | tf_op jit(solution)/shard_map/all_to_all | solution.py:181
  102.8 3.0 %home.2 = (f32[128,1024]{1,0:T(8,128)}, bf16[128,1024]{1,0:T(8,128)(2,1)}) custom-call(s32[1]{0:T(128)} %bitcast.first_ref, s32[2,128]{1,0:T(2,128)} %bitcast.65, f32[2,128]{1,0:T(2,128)} %bitcast.70, f32[4,128]{1,0:T(4,128)} %copy-done.8, bf16[8,64,1024]{2,1,0:T(8,128)(2,1)} %copy-done), custom_call_target="tpu_custom_call" | custom-call | flops 268435456 | bytes 1048576 | tf_op jit(solution)/shard_map/home/pallas_call | solution.py:123
  105.7 1.3 collective-permute-start.5
  107.1 15.6 %all-to-all-done.3.refs_3_ = bf16[8,64,1024]{2,1,0:T(8,128)(2,1)S(1)} async-done(((bf16[8,64,1024]{2,1,0:T(8,128)(2,1)}), bf16[8,64,1024]{2,1,0:T(8,128)(2,1)S(1)}, u32[]{:S(2)}, u32[]{:S(2)}) %all-to-all-start.3) | async-done | bytes 1048608 | tf_op jit(solution)/shard_map/all_to_all | solution.py:181
  122.7 1.0 copy-done.1
  123.7 2.6 %home.3 = (f32[128,1024]{1,0:T(8,128)}, bf16[128,1024]{1,0:T(8,128)(2,1)}) custom-call(s32[1]{0:T(128)} %bitcast.first_ref, s32[2,128]{1,0:T(2,128)} %bitcast.66, f32[2,128]{1,0:T(2,128)} %bitcast.71, f32[4,128]{1,0:T(4,128)} %copy-done.8, bf16[8,64,1024]{2,1,0:T(8,128)(2,1)} %copy-done.1), custom_call_target="tpu_custom_call" | custom-call | flops 134217728 | bytes 1048576 | tf_op jit(solution)/shard_map/home/pallas_call | solution.py:123
  126.3 6.3 %weight_grad.1 = bf16[1,1024,2048]{2,1,0:T(8,128)(2,1)} custom-call(s32[1]{0:T(128)} %bitcast.16.me_ref, bf16[8,2,32,1024]{3,2,1,0:T(8,128)(2,1)} %bitcast.62, bf16[8,2,32,1024]{3,2,1,0:T(8,128)(2,1)} %bitcast.72, bf16[512,1024]{1,0:T(8,128)(2,1)} %copy-done.15), custom_call_target="tpu_custom_call" | custom-call | flops 4294967296 | bytes 4194304 | tf_op jit(solution)/shard_map/weight_grad/pallas_call | solution.py:162
  132.6 0.8 add_convert_fusion.5
  133.3 6.3 %collective-permute-done.8 = bf16[128,1024]{1,0:T(8,128)(2,1)S(1)} collective-permute-done((bf16[128,1024]{1,0:T(8,128)(2,1)}, bf16[128,1024]{1,0:T(8,128)(2,1)S(1)}, u32[]{:S(2)}, u32[]{:S(2)}) %collective-permute-start.8) | collective-permute-done | bytes 262176 | tf_op jit(solution)/shard_map/ppermute | solution.py:175
  139.6 0.8 add_convert_fusion.4
  (32 shorter events, 0.1 us)
Async XLA Ops:
  0.6 39.0 %copy-start.5 = (bf16[128,1024]{1,0:T(8,128)(2,1)S(1)}, bf16[128,1024]{1,0:T(8,128)(2,1)}, u32[]{:S(2)}) copy-start(bf16[128,1024]{1,0:T(8,128)(2,1)} %refs_3_.2) | copy-start | bytes 786436
  0.6 16.4 %collective-permute-start.2 = (bf16[128,1024]{1,0:T(8,128)(2,1)}, bf16[128,1024]{1,0:T(8,128)(2,1)S(1)}, u32[]{:S(2)}, u32[]{:S(2)}) collective-permute-start(bf16[128,1024]{1,0:T(8,128)(2,1)} %refs_3_.3), channel_id=1, source_target_pairs={{0,16},{2,18},{4,20},{6,22},{8,24},{10,26},{12,28},{14,30},{16,0},... | collective-permute-start | bytes 786440 | tf_op jit(solution)/shard_map/ppermute | solution.py:175
  6.1 10.9 %collective-permute-start = (f32[4,128]{1,0:T(4,128)S(1)}, f32[4,128]{1,0:T(4,128)S(1)}, u32[]{:S(2)}, u32[]{:S(2)}) collective-permute-start(f32[4,128]{1,0:T(4,128)S(1)} %pad_maximum_fusion), channel_id=1, source_target_pairs={{0,16},{2,18},{4,20},{6,22},{8,24},{10,26},{12,28},{14,30},{16,0},... | collective-permute-start | bytes 6152 | tf_op jit(solution)/shard_map/ppermute | solution.py:175
  17.0 0.6 copy-start.8
  17.0 0.7 copy-start.7
  39.6 22.9 %collective-permute-start.3 = (bf16[512,1024]{1,0:T(8,128)(2,1)S(1)}, bf16[512,1024]{1,0:T(8,128)(2,1)S(1)}, u32[]{:S(2)}, u32[]{:S(2)}) collective-permute-start(bf16[512,1024]{1,0:T(8,128)(2,1)S(1)} %bitcast.58), channel_id=1, source_target_pairs={{1,0},{0,1},{3,2},{2,3},{5,4},{4,5},{7,6},{6,7},{9,8},{8,9},{11,10... | collective-permute-start | bytes 3145736 | tf_op jit(solution)/shard_map/ppermute | solution.py:188
  39.6 15.9 %collective-permute-start.1 = (bf16[128,1024]{1,0:T(8,128)(2,1)S(1)}, bf16[128,1024]{1,0:T(8,128)(2,1)S(1)}, u32[]{:S(2)}, u32[]{:S(2)}) collective-permute-start(bf16[128,1024]{1,0:T(8,128)(2,1)S(1)} %copy-done.5), channel_id=1, source_target_pairs={{0,16},{2,18},{4,20},{6,22},{8,24},{10,26},{12,28},{14,30},{16,0},... | collective-permute-start | bytes 786440 | tf_op jit(solution)/shard_map/ppermute | solution.py:175
  55.5 0.7 copy-start.6
  58.9 18.7 %all-to-all-start = ((bf16[8,64,1024]{2,1,0:T(8,128)(2,1)}), bf16[8,64,1024]{2,1,0:T(8,128)(2,1)S(1)}, u32[]{:S(2)}, u32[]{:S(2)}) async-start(bf16[8,64,1024]{2,1,0:T(8,128)(2,1)} %slots.2), calls=%async_computation | async-start | bytes 2097152 | tf_op jit(solution)/shard_map/all_to_all | solution.py:181
  62.5 2.2 %copy-start.12 = (bf16[1,2048,1024]{2,1,0:T(8,128)(2,1)S(1)}, bf16[1,2048,1024]{2,1,0:T(8,128)(2,1)}, u32[]{:S(2)}) copy-start(bf16[1,2048,1024]{2,1,0:T(8,128)(2,1)} %param.10) | copy-start | bytes 12582916
  64.7 2.3 %copy-start.10 = (bf16[1,2048,1024]{2,1,0:T(8,128)(2,1)S(1)}, bf16[1,2048,1024]{2,1,0:T(8,128)(2,1)}, u32[]{:S(2)}) copy-start(bf16[1,2048,1024]{2,1,0:T(8,128)(2,1)} %param.11) | copy-start | bytes 12582916
  67.0 3.7 %copy-start.16 = (f32[512,1024]{1,0:T(8,128)}, f32[512,1024]{1,0:T(8,128)S(1)}, u32[]{:S(2)}) copy-start(f32[512,1024]{1,0:T(8,128)S(1)} %fusion.4) | copy-start | bytes 6291460
  67.0 3.7 %copy-start.9 = (bf16[1,1024,2048]{2,1,0:T(8,128)(2,1)S(1)}, bf16[1,1024,2048]{2,1,0:T(8,128)(2,1)}, u32[]{:S(2)}) copy-start(bf16[1,1024,2048]{2,1,0:T(8,128)(2,1)} %param.12) | copy-start | bytes 12582916
  70.8 2.3 %copy-start.15 = (bf16[512,1024]{1,0:T(8,128)(2,1)}, bf16[512,1024]{1,0:T(8,128)(2,1)S(1)}, u32[]{:S(2)}) copy-start(bf16[512,1024]{1,0:T(8,128)(2,1)S(1)} %get-tuple-element.17.refs_2_) | copy-start | bytes 3145732
  73.1 3.2 %collective-permute-start.4 = (bf16[512,1024]{1,0:T(8,128)(2,1)}, bf16[512,1024]{1,0:T(8,128)(2,1)S(1)}, u32[]{:S(2)}, u32[]{:S(2)}) collective-permute-start(bf16[512,1024]{1,0:T(8,128)(2,1)} %fusion.32), channel_id=1, source_target_pairs={{0,1},{1,0},{2,3},{3,2},{4,5},{5,4},{6,7},{7,6},{8,9},{9,8},{10,11... | collective-permute-start | bytes 3145736 | tf_op jit(solution)/shard_map/ppermute | solution.py:194
  77.7 12.4 %copy-start.2 = (bf16[8,64,1024]{2,1,0:T(8,128)(2,1)}, bf16[8,64,1024]{2,1,0:T(8,128)(2,1)S(1)}, u32[]{:S(2)}) copy-start(bf16[8,64,1024]{2,1,0:T(8,128)(2,1)S(1)} %all-to-all-done) | copy-start | bytes 3145732
  77.7 5.5 %collective-permute-start.6 = (bf16[512,1024]{1,0:T(8,128)(2,1)S(1)}, bf16[512,1024]{1,0:T(8,128)(2,1)S(1)}, u32[]{:S(2)}, u32[]{:S(2)}) collective-permute-start(bf16[512,1024]{1,0:T(8,128)(2,1)S(1)} %bitcast.60), channel_id=1, source_target_pairs={{1,0},{0,1},{3,2},{2,3},{5,4},{4,5},{7,6},{6,7},{9,8},{8,9},{11,10... | collective-permute-start | bytes 3145736 | tf_op jit(solution)/shard_map/ppermute | solution.py:188
  78.2 19.8 %all-to-all-start.2 = ((bf16[8,64,1024]{2,1,0:T(8,128)(2,1)}), bf16[8,64,1024]{2,1,0:T(8,128)(2,1)S(1)}, u32[]{:S(2)}, u32[]{:S(2)}) async-start(bf16[8,64,1024]{2,1,0:T(8,128)(2,1)} %bitcast.8), calls=%async_computation.2 | async-start | bytes 2097152 | tf_op jit(solution)/shard_map/all_to_all | solution.py:181
  83.2 6.8 %copy-start.14 = (bf16[512,1024]{1,0:T(8,128)(2,1)}, bf16[512,1024]{1,0:T(8,128)(2,1)S(1)}, u32[]{:S(2)}) copy-start(bf16[512,1024]{1,0:T(8,128)(2,1)S(1)} %collective-permute-done.6) | copy-start | bytes 3145732
  83.2 6.8 %copy-start.11 = (bf16[1,2048,1024]{2,1,0:T(8,128)(2,1)S(1)}, bf16[1,2048,1024]{2,1,0:T(8,128)(2,1)}, u32[]{:S(2)}) copy-start(bf16[1,2048,1024]{2,1,0:T(8,128)(2,1)} %param.11) | copy-start | bytes 12582916
  90.0 2.2 %copy-start.13 = (bf16[1,2048,1024]{2,1,0:T(8,128)(2,1)S(1)}, bf16[1,2048,1024]{2,1,0:T(8,128)(2,1)}, u32[]{:S(2)}) copy-start(bf16[1,2048,1024]{2,1,0:T(8,128)(2,1)} %param.10) | copy-start | bytes 12582916
  93.5 2.7 %collective-permute-start.7 = (bf16[512,1024]{1,0:T(8,128)(2,1)S(1)}, bf16[512,1024]{1,0:T(8,128)(2,1)S(1)}, u32[]{:S(2)}, u32[]{:S(2)}) collective-permute-start(bf16[512,1024]{1,0:T(8,128)(2,1)S(1)} %add_convert_fusion.1), channel_id=1, source_target_pairs={{0,1},{1,0},{2,3},{3,2},{4,5},{5,4},{6,7},{7,6},{8,9},{9,8},{10,11... | collective-permute-start | bytes 3145736 | tf_op jit(solution)/shard_map/ppermute | solution.py:194
  98.0 4.8 %copy-start = (bf16[8,64,1024]{2,1,0:T(8,128)(2,1)}, bf16[8,64,1024]{2,1,0:T(8,128)(2,1)S(1)}, u32[]{:S(2)}) copy-start(bf16[8,64,1024]{2,1,0:T(8,128)(2,1)S(1)} %all-to-all-done.2.refs_3_) | copy-start | bytes 3145732
  98.0 24.7 %all-to-all-start.3 = ((bf16[8,64,1024]{2,1,0:T(8,128)(2,1)}), bf16[8,64,1024]{2,1,0:T(8,128)(2,1)S(1)}, u32[]{:S(2)}, u32[]{:S(2)}) async-start(bf16[8,64,1024]{2,1,0:T(8,128)(2,1)} %bitcast.15), calls=%async_computation.3 | async-start | bytes 2097152 | tf_op jit(solution)/shard_map/all_to_all | solution.py:181
  105.7 26.9 %collective-permute-start.5 = (bf16[128,1024]{1,0:T(8,128)(2,1)}, bf16[128,1024]{1,0:T(8,128)(2,1)S(1)}, u32[]{:S(2)}, u32[]{:S(2)}) collective-permute-start(bf16[128,1024]{1,0:T(8,128)(2,1)} %get-tuple-element.11), channel_id=1, source_target_pairs={{0,16},{2,18},{4,20},{6,22},{8,24},{10,26},{12,28},{14,30},{16,0},... | collective-permute-start | bytes 786440 | tf_op jit(solution)/shard_map/ppermute | solution.py:175
  122.7 1.0 copy-start.1
  126.3 13.4 %collective-permute-start.8 = (bf16[128,1024]{1,0:T(8,128)(2,1)}, bf16[128,1024]{1,0:T(8,128)(2,1)S(1)}, u32[]{:S(2)}, u32[]{:S(2)}) collective-permute-start(bf16[128,1024]{1,0:T(8,128)(2,1)} %get-tuple-element.14), channel_id=1, source_target_pairs={{0,16},{2,18},{4,20},{6,22},{8,24},{10,26},{12,28},{14,30},{16,0},... | collective-permute-start | bytes 786440 | tf_op jit(solution)/shard_map/ppermute | solution.py:175
  126.3 6.3 %copy-start.3 = (f32[128,1024]{1,0:T(8,128)S(1)}, f32[128,1024]{1,0:T(8,128)}, u32[]{:S(2)}) copy-start(f32[128,1024]{1,0:T(8,128)} %get-tuple-element.10) | copy-start | bytes 1572868
  126.3 13.4 %copy-start.4 = (f32[128,1024]{1,0:T(8,128)S(1)}, f32[128,1024]{1,0:T(8,128)}, u32[]{:S(2)}) copy-start(f32[128,1024]{1,0:T(8,128)} %get-tuple-element.13) | copy-start | bytes 1572868

commit v3 on v2

--- a/solution.py
+++ b/solution.py
@@ -235,13 +235,20 @@
     me = lax.axis_index("mp").astype(jnp.int32).reshape(1)
     near = (expert_ids.T, combine.T)
     far_tokens = over(tokens)
+    near_slots = build_slots(first, (near,), (tokens,), half, most, top, False)
     far = (over(jnp.concatenate([near[0].astype(F32), near[1]], axis=0)),)
+    near_rows = within(near_slots)
     far_grads = over(grad_out)
-    t_slots = build_slots(first, (near, far), (tokens, far_tokens), half, most, top, False)
-    t_rows = within(t_slots)
+    far_slots = build_slots(first, (far,), (far_tokens,), half, most, top, False)
+    far_rows = within(far_slots)
     grad_slots = build_slots(first, (near, far), (grad_out, far_grads), half, most, top, True)
     grads = within(grad_slots)
-    xs = gather_parts(t_rows.reshape(rows, width))
+    near_parts = gather_parts(near_rows.reshape(rows // 2, width))
+    far_parts = gather_parts(far_rows.reshape(rows // 2, width))
+    xs = [
+        jnp.concatenate([v.reshape(half, 1, most, width) for v in pair], axis=1).reshape(rows, width)
+        for pair in zip(near_parts, far_parts)
+    ]
     x = joined(xs)
     gate = dot(x, w_gate[0])
     up = dot(x, w_up[0])

time: 141 us -> 141 us (level)
  blocking collectives: 19.2 us -> 0 us
  starting transfers between devices: 22.7 us -> 34.8 us
  waiting for transfers between devices: 45.7 us -> 50.1 us
  Pallas kernels: 17.3 us -> 19 us
    all_to_all x1 -> x0, blocking collectives: 19.2 us -> none  [within(): lax.all_to_all(slots, 'expert', split_axis=0, concat_axis=0, tiled=True,...]
    all_to_all x3 -> x5, starting transfers between devices: 13.3 us -> 27.3 us  [within(): lax.all_to_all(slots, 'expert', split_axis=0, concat_axis=0, tiled=True,...]
    all_to_all x3 -> x5, waiting for transfers between devices: 16 us -> 23.7 us  [within(): lax.all_to_all(slots, 'expert', split_axis=0, concat_axis=0, tiled=True,...]
    ppermute x5, waiting for transfers between devices: 29.7 us -> 26.3 us  [over(): lax.ppermute(value, 'expert', [(j, (j + experts // 2) % experts) for j in...]
    ppermute x5, starting transfers between devices: 8.81 us -> 6.9 us  [over(): lax.ppermute(value, 'expert', [(j, (j + experts // 2) % experts) for j in...]
    pallas_call x2 -> x3, Pallas kernels: 5.45 us -> 7.16 us  [build_slots(): pl.pallas_call(functools.partial(slots_kernel, counts=[len(t) for t in ta...]
  transfers between devices with their start and end apart: 12 -> 15, of which waited for: 5 -> 6; matrix products, arithmetic and copies ran while one was open for 21% -> 21% of each run, Pallas kernels for 10% -> 12%
where the time goes in v3:
time: 141 us; the launch traced here: 140 us
  waiting for transfers between devices  50.1 us (36%)
  starting transfers between devices  34.8 us (25%)
  matrix products  23.5 us (17%)
  Pallas kernels  19 us (13%)
  other arithmetic  7.29 us (5%)
  local copies, waits for them, and re-layouts  4.72 us (3%)
    all_to_all x5, starting transfers between devices, within(): lax.all_to_all(slots, 'expert', split_axis=0, concat_axis=0, tiled=True,...  27.3 us
    ppermute x5, waiting for transfers between devices, over(): lax.ppermute(value, 'expert', [(j, (j + experts // 2) % experts) for j in...  26.3 us
    all_to_all x5, waiting for transfers between devices, within(): lax.all_to_all(slots, 'expert', split_axis=0, concat_axis=0, tiled=True,...  23.7 us
    dot_general x9, matrix products, dot(): return lax.dot_general(a, b, dims, preferred_element_type=F32)  23.5 us
    pallas_call x3, Pallas kernels, build_slots(): pl.pallas_call(functools.partial(slots_kernel, counts=[len(t) for t in ta...  7.16 us
    ppermute x5, starting transfers between devices, over(): lax.ppermute(value, 'expert', [(j, (j + experts // 2) % experts) for j in...  6.9 us
    pallas_call x1, Pallas kernels, weight_grad(): pl.pallas_call(functools.partial(weight_kernel, parts=parts, width=width,...  6.27 us
    pallas_call x2, Pallas kernels, bring_home(): pl.pallas_call(functools.partial(home_kernel, counts=[len(t) for t in tab...  5.61 us
  transfers between devices with their start and end apart: 15, of which 6 were waited for; matrix products, arithmetic and copies ran while one was open for 21% of the time, Pallas kernels for 12%

profile of v3, /device:TPU:0, one launch (start us, length us, event | category | flops | bytes accessed | tf_op | source)
XLA Modules:
  0.0 140.3 jit_solution(16032223702012578231)
XLA Ops:
  0.7 2.2 %slots.4 = bf16[8,32,1024]{2,1,0:T(8,128)(2,1)} custom-call(s32[1]{0:T(128)} %bitcast.first_ref, s32[2,128]{1,0:T(2,128)} %bitcast.76, f32[2,128]{1,0:T(2,128)} %bitcast.80, bf16[128,1024]{1,0:T(8,128)(2,1)} %refs_2_.1), custom_call_target="tpu_custom_call" | custom-call | flops 67108864 | bytes 786432 | tf_op jit(solution)/shard_map/slots/pallas_call | solution.py:80
  2.9 6.2 %all-to-all-start.1 = ((bf16[8,32,1024]{2,1,0:T(8,128)(2,1)}), bf16[8,32,1024]{2,1,0:T(8,128)(2,1)S(1)}, u32[]{:S(2)}, u32[]{:S(2)}) async-start(bf16[8,32,1024]{2,1,0:T(8,128)(2,1)} %slots.4), calls=%async_computation.1 | async-start | bytes 1048576 | tf_op jit(solution)/shard_map/all_to_all | solution.py:181
  9.1 2.6 %collective-permute-start.2 = (bf16[128,1024]{1,0:T(8,128)(2,1)}, bf16[128,1024]{1,0:T(8,128)(2,1)S(1)}, u32[]{:S(2)}, u32[]{:S(2)}) collective-permute-start(bf16[128,1024]{1,0:T(8,128)(2,1)} %refs_2_.1), channel_id=1, source_target_pairs={{0,16},{2,18},{4,20},{6,22},{8,24},{10,26},{12,28},{14,30},{16,0},... | collective-permute-start | bytes 786440 | tf_op jit(solution)/shard_map/ppermute | solution.py:175
  11.7 0.7 bitcast_convert_fusion
  12.4 0.7 pad_maximum_fusion.2
  13.1 0.3 collective-permute-start
  13.4 7.3 %collective-permute-done.refs_2_.refs_0_ = f32[4,128]{1,0:T(4,128)S(1)} collective-permute-done((f32[4,128]{1,0:T(4,128)S(1)}, f32[4,128]{1,0:T(4,128)S(1)}, u32[]{:S(2)}, u32[]{:S(2)}) %collective-permute-start) | collective-permute-done | bytes 2080 | tf_op jit(solution)/shard_map/ppermute | solution.py:175
  20.7 0.6 copy-done.8
  21.2 0.7 copy-done.7
  21.9 2.2 %slots.5 = bf16[8,32,1024]{2,1,0:T(8,128)(2,1)} custom-call(s32[1]{0:T(128)} %bitcast.first_ref, f32[4,128]{1,0:T(4,128)} %copy-done.8, bf16[128,1024]{1,0:T(8,128)(2,1)} %copy-done.7), custom_call_target="tpu_custom_call" | custom-call | flops 67108864 | bytes 786432 | tf_op jit(solution)/shard_map/slots/pallas_call | solution.py:80
  24.1 7.8 %all-to-all-start.2 = ((bf16[8,32,1024]{2,1,0:T(8,128)(2,1)}), bf16[8,32,1024]{2,1,0:T(8,128)(2,1)S(1)}, u32[]{:S(2)}, u32[]{:S(2)}) async-start(bf16[8,32,1024]{2,1,0:T(8,128)(2,1)} %slots.5), calls=%async_computation.2 | async-start | bytes 1048576 | tf_op jit(solution)/shard_map/all_to_all | solution.py:181
  31.9 7.9 %all-to-all-done.2 = bf16[8,32,1024]{2,1,0:T(8,128)(2,1)S(1)} async-done(((bf16[8,32,1024]{2,1,0:T(8,128)(2,1)}), bf16[8,32,1024]{2,1,0:T(8,128)(2,1)S(1)}, u32[]{:S(2)}, u32[]{:S(2)}) %all-to-all-start.2) | async-done | bytes 524320 | tf_op jit(solution)/shard_map/all_to_all | solution.py:181
  39.8 2.5 %collective-permute-start.1 = (bf16[128,1024]{1,0:T(8,128)(2,1)S(1)}, bf16[128,1024]{1,0:T(8,128)(2,1)S(1)}, u32[]{:S(2)}, u32[]{:S(2)}) collective-permute-start(bf16[128,1024]{1,0:T(8,128)(2,1)S(1)} %copy-done.5), channel_id=1, source_target_pairs={{0,16},{2,18},{4,20},{6,22},{8,24},{10,26},{12,28},{14,30},{16,0},... | collective-permute-start | bytes 786440 | tf_op jit(solution)/shard_map/ppermute | solution.py:175
  42.3 12.8 %collective-permute-done.1.refs_4_ = bf16[128,1024]{1,0:T(8,128)(2,1)S(1)} collective-permute-done((bf16[128,1024]{1,0:T(8,128)(2,1)S(1)}, bf16[128,1024]{1,0:T(8,128)(2,1)S(1)}, u32[]{:S(2)}, u32[]{:S(2)}) %collective-permute-start.1) | collective-permute-done | bytes 262176 | tf_op jit(solution)/shard_map/ppermute | solution.py:175
  55.1 0.7 copy-done.6
  55.8 2.8 %slots.3 = bf16[8,64,1024]{2,1,0:T(8,128)(2,1)} custom-call(s32[1]{0:T(128)} %bitcast.first_ref, s32[2,128]{1,0:T(2,128)} %bitcast.77, f32[2,128]{1,0:T(2,128)} %bitcast.82, f32[4,128]{1,0:T(4,128)} %copy-done.8, bf16[128,1024]{1,0:T(8,128)(2,1)} %refs_3_.1, bf16[128,1024]{1,0:T(8,128)(2,1)} %copy-done.6), custom_call_target="tpu_custom_call" | custom-call | flops 134217728 | bytes 1572864 | tf_op jit(solution)/shard_map/slots/pallas_call | solution.py:80
  58.5 3.6 %all-to-all-start = ((bf16[8,64,1024]{2,1,0:T(8,128)(2,1)}), bf16[8,64,1024]{2,1,0:T(8,128)(2,1)S(1)}, u32[]{:S(2)}, u32[]{:S(2)}) async-start(bf16[8,64,1024]{2,1,0:T(8,128)(2,1)} %slots.3), calls=%async_computation | async-start | bytes 2097152 | tf_op jit(solution)/shard_map/all_to_all | solution.py:181
  62.1 0.1 pad_maximum_fusion
  62.2 0.1 copy.10
  62.3 0.1 pad_maximum_fusion.1
  62.4 1.4 %fusion.10 = bf16[512,2048]{1,0:T(8,128)(2,1)S(1)} fusion(s32[]{:T(128)S(6)} %select_n.45, bf16[512,1024]{1,0:T(8,128)(2,1)S(1)} %bitcast.65, bf16[512,1024]{1,0:T(8,128)(2,1)S(1)} %bitcast.66), kind=kLoop, calls=%fused_computation.15 | loop fusion | flops 6291456 | bytes 4194308 | tf_op jit(solution)/shard_map/concatenate | solution.py:221
  63.9 0.8 copy-done.12
  64.6 2.3 %fusion.4 = f32[512,1024]{1,0:T(8,128)S(1)} fusion(bf16[512,2048]{1,0:T(8,128)(2,1)S(1)} %fusion.10, bf16[1,2048,1024]{2,1,0:T(8,128)(2,1)S(1)} %copy-done.12), kind=kOutput, calls=%fused_computation.4 | convolution fusion | flops 2147483648 | bytes 8388608 | tf_op jit(solution)/shard_map/dot_general | solution.py:216
  67.0 3.7 %multiply_convert_fusion.2 = (bf16[512,1024]{1,0:T(8,128)(2,1)S(1)}, f32[512,1024]{1,0:T(8,128)}) fusion(f32[512,1024]{1,0:T(8,128)S(1)} %fusion.4, bf16[512,2048]{1,0:T(8,128)(2,1)S(1)} %fusion.10, bf16[1,2048,1024]{2,1,0:T(8,128)(2,1)S(1)} %copy-done.10), kind=kOutput, calls=%fused_computation.40 | convolution fusion | flops 2150629376 | bytes 11534336 | tf_op jit(solution)/shard_map/dot_general | solution.py:216
  70.7 2.3 %fusion.32 = bf16[512,1024]{1,0:T(8,128)(2,1)} fusion(bf16[512,1024]{1,0:T(8,128)(2,1)S(1)} %get-tuple-element.17.refs_2_, bf16[1,1024,2048]{2,1,0:T(8,128)(2,1)S(1)} %copy-done.9, s32[]{:T(128)S(6)} %select_n.49), kind=kOutput, calls=%fused_computation.43 | convolution fusion | flops 1074266112 | bytes 4194308 | tf_op jit(solution)/shard_map/dot_general | solution.py:216
  73.0 3.2 %fusion.29 = bf16[512,1024]{1,0:T(8,128)(2,1)S(1)} fusion(bf16[512,1024]{1,0:T(8,128)(2,1)} %copy-done.15, bf16[1,1024,2048]{2,1,0:T(8,128)(2,1)} %param.12, s32[]{:T(128)S(6)} %select_n.47), kind=kOutput, calls=%fused_computation.42 | convolution fusion | flops 1074266112 | bytes 4194308 | tf_op jit(solution)/shard_map/dot_general | solution.py:216
  76.2 1.4 %add_convert_fusion.3 = bf16[512,1024]{1,0:T(8,128)(2,1)} fusion(bf16[512,1024]{1,0:T(8,128)(2,1)S(1)} %collective-permute-done.5, bf16[512,1024]{1,0:T(8,128)(2,1)S(1)} %fusion.29), kind=kLoop, calls=%fused_computation.37 | loop fusion | flops 2097152 | bytes 3145728 | tf_op jit(solution)/shard_map/convert_element_type | solution.py:203
  77.6 0.5 collective-permute-start.7
  78.1 5.0 %all-to-all-start.3 = ((bf16[8,64,1024]{2,1,0:T(8,128)(2,1)}), bf16[8,64,1024]{2,1,0:T(8,128)(2,1)S(1)}, u32[]{:S(2)}, u32[]{:S(2)}) async-start(bf16[8,64,1024]{2,1,0:T(8,128)(2,1)} %bitcast.15), calls=%async_computation.3 | async-start | bytes 2097152 | tf_op jit(solution)/shard_map/all_to_all | solution.py:181
  83.1 6.8 %multiply_convert_fusion.1 = (bf16[512,1024]{1,0:T(8,128)(2,1)S(1)}, bf16[512,1024]{1,0:T(8,128)(2,1)S(1)}) fusion(f32[512,1024]{1,0:T(8,128)} %copy-done.16, f32[512,1024]{1,0:T(8,128)} %get-tuple-element.18, bf16[1,1024,2048]{2,1,0:T(8,128)(2,1)} %param.12, s32[]{:T(128)S(6)} %select_n.45, bf16[512,1024]{1,0:T(8,128)(2,1)S(1)} %bitcast.72, ...), kind=kOutput, calls=%fused_computation.36 | convolution fusion | flops 2160590848 | bytes 12582916 | tf_op jit(solution)/shard_map/dot_general | solution.py:216
  90.0 1.3 fusion.11
  91.3 0.9 copy-done.13
  92.2 1.3 add_convert_fusion.1
  93.5 0.1 collective-permute-start.8
  93.5 1.3 fusion.15
  94.8 1.3 add_convert_fusion.2
  96.2 1.4 add_convert_fusion
  97.6 0.3 all-to-all-done.3.refs_3_
  97.9 4.8 %all-to-all-start.4 = ((bf16[8,64,1024]{2,1,0:T(8,128)(2,1)}), bf16[8,64,1024]{2,1,0:T(8,128)(2,1)S(1)}, u32[]{:S(2)}, u32[]{:S(2)}) async-start(bf16[8,64,1024]{2,1,0:T(8,128)(2,1)} %bitcast.22), calls=%async_computation.4 | async-start | bytes 2097152 | tf_op jit(solution)/shard_map/all_to_all | solution.py:181
  102.7 3.0 %home.2 = (f32[128,1024]{1,0:T(8,128)}, bf16[128,1024]{1,0:T(8,128)(2,1)}) custom-call(s32[1]{0:T(128)} %bitcast.first_ref, s32[2,128]{1,0:T(2,128)} %bitcast.78, f32[2,128]{1,0:T(2,128)} %bitcast.83, f32[4,128]{1,0:T(4,128)} %copy-done.8, bf16[8,64,1024]{2,1,0:T(8,128)(2,1)} %copy-done), custom_call_target="tpu_custom_call" | custom-call | flops 268435456 | bytes 1048576 | tf_op jit(solution)/shard_map/home/pallas_call | solution.py:123
  105.6 1.5 %collective-permute-start.6 = (bf16[128,1024]{1,0:T(8,128)(2,1)}, bf16[128,1024]{1,0:T(8,128)(2,1)S(1)}, u32[]{:S(2)}, u32[]{:S(2)}) collective-permute-start(bf16[128,1024]{1,0:T(8,128)(2,1)} %get-tuple-element.11), channel_id=1, source_target_pairs={{0,16},{2,18},{4,20},{6,22},{8,24},{10,26},{12,28},{14,30},{16,0},... | collective-permute-start | bytes 786440 | tf_op jit(solution)/shard_map/ppermute | solution.py:175
  107.2 15.4 %all-to-all-done.4.refs_3_ = bf16[8,64,1024]{2,1,0:T(8,128)(2,1)S(1)} async-done(((bf16[8,64,1024]{2,1,0:T(8,128)(2,1)}), bf16[8,64,1024]{2,1,0:T(8,128)(2,1)S(1)}, u32[]{:S(2)}, u32[]{:S(2)}) %all-to-all-start.4) | async-done | bytes 1048608 | tf_op jit(solution)/shard_map/all_to_all | solution.py:181
  122.6 1.0 copy-done.1
  123.6 2.7 %home.3 = (f32[128,1024]{1,0:T(8,128)}, bf16[128,1024]{1,0:T(8,128)(2,1)}) custom-call(s32[1]{0:T(128)} %bitcast.first_ref, s32[2,128]{1,0:T(2,128)} %bitcast.79, f32[2,128]{1,0:T(2,128)} %bitcast.84, f32[4,128]{1,0:T(4,128)} %copy-done.8, bf16[8,64,1024]{2,1,0:T(8,128)(2,1)} %copy-done.1), custom_call_target="tpu_custom_call" | custom-call | flops 134217728 | bytes 1048576 | tf_op jit(solution)/shard_map/home/pallas_call | solution.py:123
  126.2 6.3 %weight_grad.1 = bf16[1,1024,2048]{2,1,0:T(8,128)(2,1)} custom-call(s32[1]{0:T(128)} %bitcast.23.me_ref, bf16[8,2,32,1024]{3,2,1,0:T(8,128)(2,1)} %bitcast.73, bf16[8,2,32,1024]{3,2,1,0:T(8,128)(2,1)} %bitcast.85, bf16[512,1024]{1,0:T(8,128)(2,1)} %copy-done.15), custom_call_target="tpu_custom_call" | custom-call | flops 4294967296 | bytes 4194304 | tf_op jit(solution)/shard_map/weight_grad/pallas_call | solution.py:162
  132.5 0.8 add_convert_fusion.5
  133.3 6.3 %collective-permute-done.9 = bf16[128,1024]{1,0:T(8,128)(2,1)S(1)} collective-permute-done((bf16[128,1024]{1,0:T(8,128)(2,1)}, bf16[128,1024]{1,0:T(8,128)(2,1)S(1)}, u32[]{:S(2)}, u32[]{:S(2)}) %collective-permute-start.9) | collective-permute-done | bytes 262176 | tf_op jit(solution)/shard_map/ppermute | solution.py:175
  139.6 0.8 add_convert_fusion.4
  (41 shorter events, 0.1 us)
Async XLA Ops:
  0.6 39.2 %copy-start.5 = (bf16[128,1024]{1,0:T(8,128)(2,1)S(1)}, bf16[128,1024]{1,0:T(8,128)(2,1)}, u32[]{:S(2)}) copy-start(bf16[128,1024]{1,0:T(8,128)(2,1)} %refs_3_.1) | copy-start | bytes 786436
  2.9 21.2 %all-to-all-start.1 = ((bf16[8,32,1024]{2,1,0:T(8,128)(2,1)}), bf16[8,32,1024]{2,1,0:T(8,128)(2,1)S(1)}, u32[]{:S(2)}, u32[]{:S(2)}) async-start(bf16[8,32,1024]{2,1,0:T(8,128)(2,1)} %slots.4), calls=%async_computation.1 | async-start | bytes 1048576 | tf_op jit(solution)/shard_map/all_to_all | solution.py:181
  9.1 11.6 %collective-permute-start.2 = (bf16[128,1024]{1,0:T(8,128)(2,1)}, bf16[128,1024]{1,0:T(8,128)(2,1)S(1)}, u32[]{:S(2)}, u32[]{:S(2)}) collective-permute-start(bf16[128,1024]{1,0:T(8,128)(2,1)} %refs_2_.1), channel_id=1, source_target_pairs={{0,16},{2,18},{4,20},{6,22},{8,24},{10,26},{12,28},{14,30},{16,0},... | collective-permute-start | bytes 786440 | tf_op jit(solution)/shard_map/ppermute | solution.py:175
  13.1 7.6 %collective-permute-start = (f32[4,128]{1,0:T(4,128)S(1)}, f32[4,128]{1,0:T(4,128)S(1)}, u32[]{:S(2)}, u32[]{:S(2)}) collective-permute-start(f32[4,128]{1,0:T(4,128)S(1)} %pad_maximum_fusion.2), channel_id=1, source_target_pairs={{0,16},{2,18},{4,20},{6,22},{8,24},{10,26},{12,28},{14,30},{16,0},... | collective-permute-start | bytes 6152 | tf_op jit(solution)/shard_map/ppermute | solution.py:175
  20.7 0.6 copy-start.8
  21.2 0.7 copy-start.7
  24.1 15.7 %all-to-all-start.2 = ((bf16[8,32,1024]{2,1,0:T(8,128)(2,1)}), bf16[8,32,1024]{2,1,0:T(8,128)(2,1)S(1)}, u32[]{:S(2)}, u32[]{:S(2)}) async-start(bf16[8,32,1024]{2,1,0:T(8,128)(2,1)} %slots.5), calls=%async_computation.2 | async-start | bytes 1048576 | tf_op jit(solution)/shard_map/all_to_all | solution.py:181
  31.9 30.4 %collective-permute-start.3 = (bf16[256,1024]{1,0:T(8,128)(2,1)S(1)}, bf16[256,1024]{1,0:T(8,128)(2,1)S(1)}, u32[]{:S(2)}, u32[]{:S(2)}) collective-permute-start(bf16[256,1024]{1,0:T(8,128)(2,1)S(1)} %bitcast.67), channel_id=1, source_target_pairs={{1,0},{0,1},{3,2},{2,3},{5,4},{4,5},{7,6},{6,7},{9,8},{8,9},{11,10... | collective-permute-start | bytes 1572872 | tf_op jit(solution)/shard_map/ppermute | solution.py:188
  39.8 22.5 %collective-permute-start.4 = (bf16[256,1024]{1,0:T(8,128)(2,1)S(1)}, bf16[256,1024]{1,0:T(8,128)(2,1)S(1)}, u32[]{:S(2)}, u32[]{:S(2)}) collective-permute-start(bf16[256,1024]{1,0:T(8,128)(2,1)S(1)} %bitcast.69), channel_id=1, source_target_pairs={{1,0},{0,1},{3,2},{2,3},{5,4},{4,5},{7,6},{6,7},{9,8},{8,9},{11,10... | collective-permute-start | bytes 1572872 | tf_op jit(solution)/shard_map/ppermute | solution.py:188
  39.8 15.2 %collective-permute-start.1 = (bf16[128,1024]{1,0:T(8,128)(2,1)S(1)}, bf16[128,1024]{1,0:T(8,128)(2,1)S(1)}, u32[]{:S(2)}, u32[]{:S(2)}) collective-permute-start(bf16[128,1024]{1,0:T(8,128)(2,1)S(1)} %copy-done.5), channel_id=1, source_target_pairs={{0,16},{2,18},{4,20},{6,22},{8,24},{10,26},{12,28},{14,30},{16,0},... | collective-permute-start | bytes 786440 | tf_op jit(solution)/shard_map/ppermute | solution.py:175
  55.1 0.7 copy-start.6
  58.5 19.0 %all-to-all-start = ((bf16[8,64,1024]{2,1,0:T(8,128)(2,1)}), bf16[8,64,1024]{2,1,0:T(8,128)(2,1)S(1)}, u32[]{:S(2)}, u32[]{:S(2)}) async-start(bf16[8,64,1024]{2,1,0:T(8,128)(2,1)} %slots.3), calls=%async_computation | async-start | bytes 2097152 | tf_op jit(solution)/shard_map/all_to_all | solution.py:181
  62.4 2.2 %copy-start.12 = (bf16[1,2048,1024]{2,1,0:T(8,128)(2,1)S(1)}, bf16[1,2048,1024]{2,1,0:T(8,128)(2,1)}, u32[]{:S(2)}) copy-start(bf16[1,2048,1024]{2,1,0:T(8,128)(2,1)} %param.10) | copy-start | bytes 12582916
  64.6 2.3 %copy-start.10 = (bf16[1,2048,1024]{2,1,0:T(8,128)(2,1)S(1)}, bf16[1,2048,1024]{2,1,0:T(8,128)(2,1)}, u32[]{:S(2)}) copy-start(bf16[1,2048,1024]{2,1,0:T(8,128)(2,1)} %param.11) | copy-start | bytes 12582916
  67.0 3.7 %copy-start.16 = (f32[512,1024]{1,0:T(8,128)}, f32[512,1024]{1,0:T(8,128)S(1)}, u32[]{:S(2)}) copy-start(f32[512,1024]{1,0:T(8,128)S(1)} %fusion.4) | copy-start | bytes 6291460
  67.0 3.7 %copy-start.9 = (bf16[1,1024,2048]{2,1,0:T(8,128)(2,1)S(1)}, bf16[1,1024,2048]{2,1,0:T(8,128)(2,1)}, u32[]{:S(2)}) copy-start(bf16[1,1024,2048]{2,1,0:T(8,128)(2,1)} %param.12) | copy-start | bytes 12582916
  70.7 2.3 %copy-start.15 = (bf16[512,1024]{1,0:T(8,128)(2,1)}, bf16[512,1024]{1,0:T(8,128)(2,1)S(1)}, u32[]{:S(2)}) copy-start(bf16[512,1024]{1,0:T(8,128)(2,1)S(1)} %get-tuple-element.17.refs_2_) | copy-start | bytes 3145732
  73.0 3.2 %collective-permute-start.5 = (bf16[512,1024]{1,0:T(8,128)(2,1)}, bf16[512,1024]{1,0:T(8,128)(2,1)S(1)}, u32[]{:S(2)}, u32[]{:S(2)}) collective-permute-start(bf16[512,1024]{1,0:T(8,128)(2,1)} %fusion.32), channel_id=1, source_target_pairs={{0,1},{1,0},{2,3},{3,2},{4,5},{5,4},{6,7},{7,6},{8,9},{9,8},{10,11... | collective-permute-start | bytes 3145736 | tf_op jit(solution)/shard_map/ppermute | solution.py:194
  77.6 12.4 %copy-start.2 = (bf16[8,64,1024]{2,1,0:T(8,128)(2,1)}, bf16[8,64,1024]{2,1,0:T(8,128)(2,1)S(1)}, u32[]{:S(2)}) copy-start(bf16[8,64,1024]{2,1,0:T(8,128)(2,1)S(1)} %all-to-all-done) | copy-start | bytes 3145732
  77.6 5.5 %collective-permute-start.7 = (bf16[512,1024]{1,0:T(8,128)(2,1)S(1)}, bf16[512,1024]{1,0:T(8,128)(2,1)S(1)}, u32[]{:S(2)}, u32[]{:S(2)}) collective-permute-start(bf16[512,1024]{1,0:T(8,128)(2,1)S(1)} %bitcast.71), channel_id=1, source_target_pairs={{1,0},{0,1},{3,2},{2,3},{5,4},{4,5},{7,6},{6,7},{9,8},{8,9},{11,10... | collective-permute-start | bytes 3145736 | tf_op jit(solution)/shard_map/ppermute | solution.py:188
  78.1 19.8 %all-to-all-start.3 = ((bf16[8,64,1024]{2,1,0:T(8,128)(2,1)}), bf16[8,64,1024]{2,1,0:T(8,128)(2,1)S(1)}, u32[]{:S(2)}, u32[]{:S(2)}) async-start(bf16[8,64,1024]{2,1,0:T(8,128)(2,1)} %bitcast.15), calls=%async_computation.3 | async-start | bytes 2097152 | tf_op jit(solution)/shard_map/all_to_all | solution.py:181
  83.1 6.8 %copy-start.14 = (bf16[512,1024]{1,0:T(8,128)(2,1)}, bf16[512,1024]{1,0:T(8,128)(2,1)S(1)}, u32[]{:S(2)}) copy-start(bf16[512,1024]{1,0:T(8,128)(2,1)S(1)} %collective-permute-done.7) | copy-start | bytes 3145732
  83.1 6.8 %copy-start.11 = (bf16[1,2048,1024]{2,1,0:T(8,128)(2,1)S(1)}, bf16[1,2048,1024]{2,1,0:T(8,128)(2,1)}, u32[]{:S(2)}) copy-start(bf16[1,2048,1024]{2,1,0:T(8,128)(2,1)} %param.11) | copy-start | bytes 12582916
  90.0 2.2 %copy-start.13 = (bf16[1,2048,1024]{2,1,0:T(8,128)(2,1)S(1)}, bf16[1,2048,1024]{2,1,0:T(8,128)(2,1)}, u32[]{:S(2)}) copy-start(bf16[1,2048,1024]{2,1,0:T(8,128)(2,1)} %param.10) | copy-start | bytes 12582916
  93.5 2.7 %collective-permute-start.8 = (bf16[512,1024]{1,0:T(8,128)(2,1)S(1)}, bf16[512,1024]{1,0:T(8,128)(2,1)S(1)}, u32[]{:S(2)}, u32[]{:S(2)}) collective-permute-start(bf16[512,1024]{1,0:T(8,128)(2,1)S(1)} %add_convert_fusion.1), channel_id=1, source_target_pairs={{0,1},{1,0},{2,3},{3,2},{4,5},{5,4},{6,7},{7,6},{8,9},{9,8},{10,11... | collective-permute-start | bytes 3145736 | tf_op jit(solution)/shard_map/ppermute | solution.py:194
  97.9 4.8 %copy-start = (bf16[8,64,1024]{2,1,0:T(8,128)(2,1)}, bf16[8,64,1024]{2,1,0:T(8,128)(2,1)S(1)}, u32[]{:S(2)}) copy-start(bf16[8,64,1024]{2,1,0:T(8,128)(2,1)S(1)} %all-to-all-done.3.refs_3_) | copy-start | bytes 3145732
  97.9 24.7 %all-to-all-start.4 = ((bf16[8,64,1024]{2,1,0:T(8,128)(2,1)}), bf16[8,64,1024]{2,1,0:T(8,128)(2,1)S(1)}, u32[]{:S(2)}, u32[]{:S(2)}) async-start(bf16[8,64,1024]{2,1,0:T(8,128)(2,1)} %bitcast.22), calls=%async_computation.4 | async-start | bytes 2097152 | tf_op jit(solution)/shard_map/all_to_all | solution.py:181
  105.6 26.9 %collective-permute-start.6 = (bf16[128,1024]{1,0:T(8,128)(2,1)}, bf16[128,1024]{1,0:T(8,128)(2,1)S(1)}, u32[]{:S(2)}, u32[]{:S(2)}) collective-permute-start(bf16[128,1024]{1,0:T(8,128)(2,1)} %get-tuple-element.11), channel_id=1, source_target_pairs={{0,16},{2,18},{4,20},{6,22},{8,24},{10,26},{12,28},{14,30},{16,0},... | collective-permute-start | bytes 786440 | tf_op jit(solution)/shard_map/ppermute | solution.py:175
  122.6 1.0 copy-start.1
  126.2 13.4 %collective-permute-start.9 = (bf16[128,1024]{1,0:T(8,128)(2,1)}, bf16[128,1024]{1,0:T(8,128)(2,1)S(1)}, u32[]{:S(2)}, u32[]{:S(2)}) collective-permute-start(bf16[128,1024]{1,0:T(8,128)(2,1)} %get-tuple-element.14), channel_id=1, source_target_pairs={{0,16},{2,18},{4,20},{6,22},{8,24},{10,26},{12,28},{14,30},{16,0},... | collective-permute-start | bytes 786440 | tf_op jit(solution)/shard_map/ppermute | solution.py:175
  126.2 6.3 %copy-start.3 = (f32[128,1024]{1,0:T(8,128)S(1)}, f32[128,1024]{1,0:T(8,128)}, u32[]{:S(2)}) copy-start(f32[128,1024]{1,0:T(8,128)} %get-tuple-element.10) | copy-start | bytes 1572868
  126.2 13.4 %copy-start.4 = (f32[128,1024]{1,0:T(8,128)S(1)}, f32[128,1024]{1,0:T(8,128)}, u32[]{:S(2)}) copy-start(f32[128,1024]{1,0:T(8,128)} %get-tuple-element.13) | copy-start | bytes 1572868

commit v4 on v3

--- a/solution.py
+++ b/solution.py
@@ -132,6 +132,34 @@
     )(first, *flat, back)
 
 
+def selectors_kernel(first_ref, *refs, counts, most, top):
+    groups, outs = take(refs, counts)
+    experts = outs[0].shape[0]
+    first = first_ref[0]
+    for s, group in enumerate(groups):
+        ids, _ = split_table(group, top)
+        count = ids.shape[1]
+        _, named, rank = ranks(ids, first, experts)
+        place = jnp.where(named, rank, -1.0)
+        want = lax.broadcasted_iota(jnp.int32, (experts, most, count), 1).astype(F32)
+        select = jnp.where(want == place[:, None, :], 1.0, 0.0).astype(BF16)
+        for at in range(len(groups)):
+            outs[s][:, at * most : (at + 1) * most, :] = select if at == s else jnp.zeros_like(select)
+
+
+def selectors(first, tables, experts, most, count, top):
+    flat = [t for table in tables for t in table]
+    shape = jax.ShapeDtypeStruct((experts, len(tables) * most, count), BF16)
+    result = pl.pallas_call(
+        functools.partial(selectors_kernel, counts=[len(t) for t in tables], most=most, top=top),
+        in_specs=[SMEM] + [VMEM] * len(flat),
+        out_specs=[VMEM] * len(tables),
+        out_shape=[shape] * len(tables),
+        name="selectors",
+    )(first, *flat)
+    return [r.reshape(-1, count) for r in result]
+
+
 def blocks(hidden_width):
     return 256 if hidden_width % 256 == 0 else hidden_width
 
@@ -172,7 +200,9 @@
 
 def over(value):
     experts = lax.axis_size("expert")
-    return lax.ppermute(value, "expert", [(j, (j + experts // 2) % experts) for j in range(experts)])
+    flip = experts // 2 + (experts // 4 if experts & (experts - 1) == 0 else 0)
+    pairs = [(j, j ^ flip if experts & (experts - 1) == 0 else (j + flip) % experts) for j in range(experts)]
+    return lax.ppermute(value, "expert", pairs)
 
 
 def within(slots):
@@ -212,6 +242,10 @@
     ]
 
 
+def in_vmem(value):
+    return pltpu.with_memory_space_constraint(value, pltpu.VMEM)
+
+
 def dot(a, b, dims=(((1,), (0,)), ((), ()))):
     return lax.dot_general(a, b, dims, preferred_element_type=F32)
 
@@ -230,7 +264,8 @@
     half = expert_count // 2
     width = tokens.shape[1]
     rows = 2 * half * most
-    gates, ups, downs = rank_slices(w_gate[0], 0), rank_slices(w_up[0], 0), rank_slices(w_down[0], 1)
+    gates, ups = rank_slices(w_gate[0], 0), rank_slices(w_up[0], 0)
+    downs = list(lax.optimization_barrier(tuple(rank_slices(w_down[0], 1))))
     first = ((lax.axis_index("expert") // half) * half).astype(jnp.int32).reshape(1)
     me = lax.axis_index("mp").astype(jnp.int32).reshape(1)
     near = (expert_ids.T, combine.T)
@@ -239,9 +274,9 @@
     far = (over(jnp.concatenate([near[0].astype(F32), near[1]], axis=0)),)
     near_rows = within(near_slots)
     far_grads = over(grad_out)
-    far_slots = build_slots(first, (far,), (far_tokens,), half, most, top, False)
+    far_slots = build_slots(first, (far,), (in_vmem(far_tokens),), half, most, top, False)
     far_rows = within(far_slots)
-    grad_slots = build_slots(first, (near, far), (grad_out, far_grads), half, most, top, True)
+    grad_slots = build_slots(first, (near, far), (grad_out, in_vmem(far_grads)), half, most, top, True)
     grads = within(grad_slots)
     near_parts = gather_parts(near_rows.reshape(rows // 2, width))
     far_parts = gather_parts(far_rows.reshape(rows // 2, width))
@@ -254,6 +289,9 @@
     up = dot(x, w_up[0])
     sig = jax.nn.sigmoid(gate)
     hidden = (gate * sig * up).astype(BF16)
+    by_up = (gate * sig).astype(BF16)
+    by_gate = (up * sig * (1.0 + gate * (1.0 - sig))).astype(BF16)
+    hidden, by_up, by_gate = lax.optimization_barrier((hidden, by_up, by_gate))
     outs = [dot(hidden, w).astype(BF16) for w in reversed(downs)][::-1]
     outs[0] = lax.optimization_barrier(outs[0])
     out_given = give_parts(outs)
@@ -266,10 +304,10 @@
     out_over = over(out_far)
     output = (out_near + out_over.astype(F32)).astype(BF16)
     gs = gather_parts(grads.reshape(rows, width))
-    g = joined(gs)
+    g = lax.optimization_barrier(joined(gs))
     grad_hidden = dot(g, w_down[0], NT)
-    grad_up = (grad_hidden * gate * sig).astype(BF16)
-    grad_gate = (grad_hidden * up * sig * (1.0 + gate * (1.0 - sig))).astype(BF16)
+    grad_up = (grad_hidden * by_up.astype(F32)).astype(BF16)
+    grad_gate = (grad_hidden * by_gate.astype(F32)).astype(BF16)
     terms = []
     for k in reversed(range(len(gs))):
         terms.append((dot(grad_gate, gates[k], NT) + dot(grad_up, ups[k], NT)).astype(BF16))
@@ -278,7 +316,10 @@
     given = give_parts(terms)
     down_grad = weight_grad(me, [g.reshape(half, 2, most, width) for g in gs], (hidden,))
     grad_back = within(added(given).reshape(half, 2 * most, width))
-    grad_near, grad_far = bring_home(first, (near, far), grad_back, (0, 1), (F32, BF16), row_count, most, top, False)
+    near_select, far_select = selectors(first, (near, far), half, most, row_count, top)
+    grad_back = grad_back.reshape(rows, width)
+    grad_far = dot(far_select, grad_back, TN).astype(BF16)
+    grad_near = dot(near_select, grad_back, TN)
     grad_over = over(grad_far)
     grad_tokens = (grad_near + grad_over.astype(F32)).astype(BF16)
     return output, grad_tokens, down_grad

time: 141 us -> 128 us (0.908)
  the two profiles are of different devices: /device:TPU:0 before, /device:TPU:8 now
where the time goes in v4:
time: 128 us; the launch traced here: 127 us
  waiting for transfers between devices  43.8 us (34%)
  starting transfers between devices  29 us (23%)
  matrix products  18.7 us (15%)
  Pallas kernels  17.5 us (14%)
  other arithmetic  9.14 us (7%)
  local copies, waits for them, and re-layouts  8 us (6%)
    ppermute x5, waiting for transfers between devices, over(): return lax.ppermute(value, 'expert', pairs)  25.3 us
    all_to_all x5, starting transfers between devices, within(): lax.all_to_all(slots, 'expert', split_axis=0, concat_axis=0, tiled=True,...  24.6 us
    dot_general x11, matrix products, dot(): return lax.dot_general(a, b, dims, preferred_element_type=F32)  18.7 us
    all_to_all x5, waiting for transfers between devices, within(): lax.all_to_all(slots, 'expert', split_axis=0, concat_axis=0, tiled=True,...  17.7 us
    pallas_call x3, Pallas kernels, build_slots(): pl.pallas_call(functools.partial(slots_kernel, counts=[len(t) for t in ta...  6.78 us
    pallas_call x1, Pallas kernels, weight_grad(): pl.pallas_call(functools.partial(weight_kernel, parts=parts, width=width,...  6.23 us
    dynamic_slice x1, local copies, waits for them, and re-layouts, rank_slices(): lax.dynamic_slice_in_dim(weight, (me + k) % parts * width, width, axis=axis)  4.74 us
    ppermute x5, starting transfers between devices, over(): return lax.ppermute(value, 'expert', pairs)  4.13 us
  transfers between devices with their start and end apart: 15, of which 7 were waited for; matrix products, arithmetic and copies ran while one was open for 25% of the time, Pallas kernels for 12%

profile of v4, /device:TPU:8, one launch (start us, length us, event | category | flops | bytes accessed | tf_op | source)
XLA Modules:
  0.0 127.2 jit_solution(6204082730783595091)
XLA Ops:
  0.7 2.2 %slots.4 = bf16[8,32,1024]{2,1,0:T(8,128)(2,1)} custom-call(s32[1]{0:T(128)} %bitcast.first_ref, s32[2,128]{1,0:T(2,128)} %bitcast.81, f32[2,128]{1,0:T(2,128)} %bitcast.85, bf16[128,1024]{1,0:T(8,128)(2,1)} %refs_2_.1), custom_call_target="tpu_custom_call" | custom-call | flops 67108864 | bytes 786432 | tf_op jit(solution)/shard_map/slots/pallas_call | solution.py:80
  2.9 5.2 %all-to-all-start.1 = ((bf16[8,32,1024]{2,1,0:T(8,128)(2,1)}), bf16[8,32,1024]{2,1,0:T(8,128)(2,1)S(1)}, u32[]{:S(2)}, u32[]{:S(2)}) async-start(bf16[8,32,1024]{2,1,0:T(8,128)(2,1)} %slots.4), calls=%async_computation.1 | async-start | bytes 1048576 | tf_op jit(solution)/shard_map/all_to_all | solution.py:211
  8.1 1.1 collective-permute-start.2
  9.2 0.7 bitcast_convert_fusion
  9.9 0.7 pad_maximum_fusion.2
  10.6 0.9 collective-permute-start
  11.5 9.0 %collective-permute-done.refs_2_.refs_0_ = f32[4,128]{1,0:T(4,128)S(1)} collective-permute-done((f32[4,128]{1,0:T(4,128)S(1)}, f32[4,128]{1,0:T(4,128)S(1)}, u32[]{:S(2)}, u32[]{:S(2)}) %collective-permute-start) | collective-permute-done | bytes 2080 | tf_op jit(solution)/shard_map/ppermute | solution.py:205
  20.5 0.6 copy-done.10
  21.1 1.9 %slots.5 = bf16[8,32,1024]{2,1,0:T(8,128)(2,1)} custom-call(s32[1]{0:T(128)} %bitcast.first_ref, f32[4,128]{1,0:T(4,128)} %copy-done.10, bf16[128,1024]{1,0:T(8,128)(2,1)S(1)} %collective-permute-done.2.refs_1_), custom_call_target="tpu_custom_call" | custom-call | flops 67108864 | bytes 786432 | tf_op jit(solution)/shard_map/slots/pallas_call | solution.py:80
  22.9 6.9 %all-to-all-start.2 = ((bf16[8,32,1024]{2,1,0:T(8,128)(2,1)}), bf16[8,32,1024]{2,1,0:T(8,128)(2,1)S(1)}, u32[]{:S(2)}, u32[]{:S(2)}) async-start(bf16[8,32,1024]{2,1,0:T(8,128)(2,1)} %slots.5), calls=%async_computation.2 | async-start | bytes 1048576 | tf_op jit(solution)/shard_map/all_to_all | solution.py:211
  29.9 7.2 %all-to-all-done.2 = bf16[8,32,1024]{2,1,0:T(8,128)(2,1)S(1)} async-done(((bf16[8,32,1024]{2,1,0:T(8,128)(2,1)}), bf16[8,32,1024]{2,1,0:T(8,128)(2,1)S(1)}, u32[]{:S(2)}, u32[]{:S(2)}) %all-to-all-start.2) | async-done | bytes 524320 | tf_op jit(solution)/shard_map/all_to_all | solution.py:211
  37.2 4.7 %dynamic-slice_bitcast_fusion = (bf16[1024,1024]{1,0:T(8,128)(2,1)}, bf16[1024,1024]{1,0:T(8,128)(2,1)}) fusion(bf16[1,1024,2048]{2,1,0:T(8,128)(2,1)} %param.12, s32[]{:T(128)S(6)} %select_n.49, s32[]{:T(128)S(6)} %select_n.47), kind=kLoop, calls=%fused_computation.34 | loop fusion | bytes 8388616 | tf_op jit(solution)/shard_map/dynamic_slice | solution.py:241
  41.9 9.6 %collective-permute-done.1.refs_4_ = bf16[128,1024]{1,0:T(8,128)(2,1)S(1)} collective-permute-done((bf16[128,1024]{1,0:T(8,128)(2,1)S(1)}, bf16[128,1024]{1,0:T(8,128)(2,1)S(1)}, u32[]{:S(2)}, u32[]{:S(2)}) %collective-permute-start.1) | collective-permute-done | bytes 262176 | tf_op jit(solution)/shard_map/ppermute | solution.py:205
  51.4 2.7 %slots.3 = bf16[8,64,1024]{2,1,0:T(8,128)(2,1)} custom-call(s32[1]{0:T(128)} %bitcast.first_ref, s32[2,128]{1,0:T(2,128)} %bitcast.82, f32[2,128]{1,0:T(2,128)} %bitcast.87, f32[4,128]{1,0:T(4,128)} %copy-done.10, bf16[128,1024]{1,0:T(8,128)(2,1)} %refs_3_.1, bf16[128,1024]{1,0:T(8,128)(2,1)S(1)} %collective-permute-done.1.refs_4_), custom_call_target="tpu_custom_call" | custom-call | flops 134217728 | bytes 1572864 | tf_op jit(solution)/shard_map/slots/pallas_call | solution.py:80
  54.1 3.5 %all-to-all-start = ((bf16[8,64,1024]{2,1,0:T(8,128)(2,1)}), bf16[8,64,1024]{2,1,0:T(8,128)(2,1)S(1)}, u32[]{:S(2)}, u32[]{:S(2)}) async-start(bf16[8,64,1024]{2,1,0:T(8,128)(2,1)} %slots.3), calls=%async_computation | async-start | bytes 2097152 | tf_op jit(solution)/shard_map/all_to_all | solution.py:211
  57.9 0.1 pad_maximum_fusion.1
  58.0 1.4 %fusion.9 = bf16[512,2048]{1,0:T(8,128)(2,1)S(1)} fusion(s32[]{:T(128)S(6)} %select_n.45, bf16[512,1024]{1,0:T(8,128)(2,1)S(1)} %bitcast.73, bf16[512,1024]{1,0:T(8,128)(2,1)S(1)} %bitcast.74), kind=kLoop, calls=%fused_computation.15 | loop fusion | flops 6291456 | bytes 4194308 | tf_op jit(solution)/shard_map/concatenate | solution.py:255
  59.4 0.8 copy-done.3
  60.2 2.3 %fusion.2 = f32[512,1024]{1,0:T(8,128)S(1)} fusion(bf16[512,2048]{1,0:T(8,128)(2,1)S(1)} %fusion.9, bf16[1,2048,1024]{2,1,0:T(8,128)(2,1)S(1)} %copy-done.3), kind=kOutput, calls=%fused_computation.2 | convolution fusion | flops 2147483648 | bytes 8388608 | tf_op jit(solution)/shard_map/dot_general | solution.py:250
  62.5 4.1 %multiply_convert_fusion.2 = (bf16[512,1024]{1,0:T(8,128)(2,1)}, bf16[512,1024]{1,0:T(8,128)(2,1)S(1)}, bf16[512,1024]{1,0:T(8,128)(2,1)S(1)}) fusion(f32[512,1024]{1,0:T(8,128)S(1)} %fusion.2, bf16[512,2048]{1,0:T(8,128)(2,1)S(1)} %fusion.9, bf16[1,2048,1024]{2,1,0:T(8,128)(2,1)S(1)} %copy-done.11), kind=kOutput, calls=%fused_computation.36 | convolution fusion | flops 2154299392 | bytes 11534336 | tf_op jit(solution)/shard_map/dot_general | solution.py:250
  66.6 1.3 convolution_convert_fusion
  67.9 0.6 copy-done.5
  68.6 1.3 convolution_convert_fusion.1
  69.8 0.7 collective-permute-done.5
  70.6 1.4 %add_convert_fusion.3 = bf16[512,1024]{1,0:T(8,128)(2,1)} fusion(bf16[512,1024]{1,0:T(8,128)(2,1)S(1)} %collective-permute-done.5, bf16[512,1024]{1,0:T(8,128)(2,1)S(1)} %convolution_convert_fusion.1), kind=kLoop, calls=%fused_computation.33 | loop fusion | flops 2097152 | bytes 3145728 | tf_op jit(solution)/shard_map/convert_element_type | solution.py:233
  72.0 0.1 collective-permute-start.7
  72.1 4.9 %all-to-all-start.3 = ((bf16[8,64,1024]{2,1,0:T(8,128)(2,1)}), bf16[8,64,1024]{2,1,0:T(8,128)(2,1)S(1)}, u32[]{:S(2)}, u32[]{:S(2)}) async-start(bf16[8,64,1024]{2,1,0:T(8,128)(2,1)} %bitcast.15), calls=%async_computation.3 | async-start | bytes 2097152 | tf_op jit(solution)/shard_map/all_to_all | solution.py:211
  77.0 2.6 %fusion.7 = bf16[512,2048]{1,0:T(8,128)(2,1)S(1)} fusion(s32[]{:T(128)S(6)} %select_n.45, bf16[512,1024]{1,0:T(8,128)(2,1)S(1)} %bitcast.71, bf16[512,1024]{1,0:T(8,128)(2,1)} %collective-permute-done.7), kind=kLoop, calls=%fused_computation.13 | loop fusion | flops 6291456 | bytes 4194308 | tf_op jit(solution)/shard_map/concatenate | solution.py:255
  79.7 2.4 %fusion = f32[512,1024]{1,0:T(8,128)S(1)} fusion(bf16[512,2048]{1,0:T(8,128)(2,1)S(1)} %fusion.7, bf16[1,1024,2048]{2,1,0:T(8,128)(2,1)S(1)} %copy-done.1), kind=kOutput, calls=%fused_computation | convolution fusion | flops 2147483648 | bytes 8388608 | tf_op jit(solution)/shard_map/dot_general | solution.py:250
  82.1 1.3 %fusion.10 = f32[512,1024]{1,0:T(8,128)S(1)} fusion(bf16[1,2048,1024]{2,1,0:T(8,128)(2,1)S(1)} %copy-done.4, s32[]{:T(128)S(6)} %select_n.49, f32[512,1024]{1,0:T(8,128)S(1)} %fusion, bf16[512,1024]{1,0:T(8,128)(2,1)S(1)} %get-tuple-element.23), kind=kOutput, calls=%fused_computation.16 | convolution fusion | flops 1075314688 | bytes 7340036 | tf_op jit(solution)/shard_map/dot_general | solution.py:250
  83.4 0.9 copy-done.12
  84.2 0.3 copy-done.13
  84.5 1.3 %add_convert_fusion.1 = bf16[512,1024]{1,0:T(8,128)(2,1)S(1)} fusion(f32[512,1024]{1,0:T(8,128)S(1)} %fusion.10, bf16[1,2048,1024]{2,1,0:T(8,128)(2,1)S(1)} %copy-done.12, s32[]{:T(128)S(6)} %select_n.49, f32[512,1024]{1,0:T(8,128)S(1)} %fusion, bf16[512,1024]{1,0:T(8,128)(2,1)S(1)} %copy-done.13), kind=kOutput, calls=%fused_computation.25 | convolution fusion | flops 1076363264 | bytes 8388612 | tf_op jit(solution)/shard_map/dot_general | solution.py:250
  85.9 1.3 %fusion.14 = f32[512,1024]{1,0:T(8,128)S(1)} fusion(bf16[1,2048,1024]{2,1,0:T(8,128)(2,1)S(1)} %copy-done.4, s32[]{:T(128)S(6)} %select_n.47, f32[512,1024]{1,0:T(8,128)S(1)} %fusion, bf16[512,1024]{1,0:T(8,128)(2,1)S(1)} %get-tuple-element.23), kind=kOutput, calls=%fused_computation.20 | convolution fusion | flops 1075314688 | bytes 7340036 | tf_op jit(solution)/shard_map/dot_general | solution.py:250
  87.2 1.3 %add_convert_fusion.2 = bf16[512,1024]{1,0:T(8,128)(2,1)S(1)} fusion(f32[512,1024]{1,0:T(8,128)S(1)} %fusion.14, bf16[1,2048,1024]{2,1,0:T(8,128)(2,1)S(1)} %copy-done.12, s32[]{:T(128)S(6)} %select_n.47, f32[512,1024]{1,0:T(8,128)S(1)} %fusion, bf16[512,1024]{1,0:T(8,128)(2,1)S(1)} %copy-done.13), kind=kOutput, calls=%fused_computation.28 | convolution fusion | flops 1076363264 | bytes 8388612 | tf_op jit(solution)/shard_map/dot_general | solution.py:250
  88.6 1.4 %add_convert_fusion = bf16[512,1024]{1,0:T(8,128)(2,1)} fusion(bf16[512,1024]{1,0:T(8,128)(2,1)S(1)} %collective-permute-done.8, bf16[512,1024]{1,0:T(8,128)(2,1)S(1)} %add_convert_fusion.2), kind=kLoop, calls=%fused_computation.24 | loop fusion | flops 2097152 | bytes 3145728 | tf_op jit(solution)/shard_map/convert_element_type | solution.py:233
  89.9 1.5 %all-to-all-done.3.refs_3_ = bf16[8,64,1024]{2,1,0:T(8,128)(2,1)S(1)} async-done(((bf16[8,64,1024]{2,1,0:T(8,128)(2,1)}), bf16[8,64,1024]{2,1,0:T(8,128)(2,1)S(1)}, u32[]{:S(2)}, u32[]{:S(2)}) %all-to-all-start.3) | async-done | bytes 1048608 | tf_op jit(solution)/shard_map/all_to_all | solution.py:211
  91.5 4.1 %all-to-all-start.4 = ((bf16[8,64,1024]{2,1,0:T(8,128)(2,1)}), bf16[8,64,1024]{2,1,0:T(8,128)(2,1)S(1)}, u32[]{:S(2)}, u32[]{:S(2)}) async-start(bf16[8,64,1024]{2,1,0:T(8,128)(2,1)} %bitcast.22), calls=%async_computation.4 | async-start | bytes 2097152 | tf_op jit(solution)/shard_map/all_to_all | solution.py:211
  95.6 1.6 %selectors.1 = (bf16[8,64,128]{2,1,0:T(8,128)(2,1)}, bf16[8,64,128]{2,1,0:T(8,128)(2,1)}) custom-call(s32[1]{0:T(128)} %bitcast.first_ref, s32[2,128]{1,0:T(2,128)} %bitcast.83, f32[2,128]{1,0:T(2,128)} %bitcast.88, f32[4,128]{1,0:T(4,128)} %copy-done.10), custom_call_target="tpu_custom_call" | custom-call | tf_op jit(solution)/shard_map/selectors/pallas_call | solution.py:153
  97.1 2.9 %home.1 = (f32[128,1024]{1,0:T(8,128)}, bf16[128,1024]{1,0:T(8,128)(2,1)}) custom-call(s32[1]{0:T(128)} %bitcast.first_ref, s32[2,128]{1,0:T(2,128)} %bitcast.84, f32[2,128]{1,0:T(2,128)} %bitcast.89, f32[4,128]{1,0:T(4,128)} %copy-done.10, bf16[8,64,1024]{2,1,0:T(8,128)(2,1)} %copy-done.2), custom_call_target="tpu_custom_call" | custom-call | flops 268435456 | bytes 1048576 | tf_op jit(solution)/shard_map/home/pallas_call | solution.py:123
  100.1 0.6 collective-permute-start.6
  100.7 9.0 %all-to-all-done.4 = bf16[8,64,1024]{2,1,0:T(8,128)(2,1)S(1)} async-done(((bf16[8,64,1024]{2,1,0:T(8,128)(2,1)}), bf16[8,64,1024]{2,1,0:T(8,128)(2,1)S(1)}, u32[]{:S(2)}, u32[]{:S(2)}) %all-to-all-start.4) | async-done | bytes 1048608 | tf_op jit(solution)/shard_map/all_to_all | solution.py:211
  109.6 1.2 fusion.29
  110.9 1.5 %collective-permute-start.9 = (bf16[128,1024]{1,0:T(8,128)(2,1)S(1)}, bf16[128,1024]{1,0:T(8,128)(2,1)S(1)}, u32[]{:S(2)}, u32[]{:S(2)}) collective-permute-start(bf16[128,1024]{1,0:T(8,128)(2,1)S(1)} %fusion.29), channel_id=1, source_target_pairs={{0,24},{2,26},{4,28},{6,30},{8,16},{10,18},{12,20},{14,22},{16,8},... | collective-permute-start | bytes 786440 | tf_op jit(solution)/shard_map/ppermute | solution.py:205
  112.4 6.2 %weight_grad.1 = bf16[1,1024,2048]{2,1,0:T(8,128)(2,1)} custom-call(s32[1]{0:T(128)} %bitcast.25.me_ref, bf16[8,2,32,1024]{3,2,1,0:T(8,128)(2,1)} %bitcast.72, bf16[8,2,32,1024]{3,2,1,0:T(8,128)(2,1)} %bitcast.27.refs_1_, bf16[512,1024]{1,0:T(8,128)(2,1)} %copy-done.14), custom_call_target="tpu_custom_call" | custom-call | flops 4294967296 | bytes 4194304 | tf_op jit(solution)/shard_map/weight_grad/pallas_call | solution.py:190
  118.6 0.8 add_convert_fusion.4
  119.4 6.7 %collective-permute-done.9 = bf16[128,1024]{1,0:T(8,128)(2,1)S(1)} collective-permute-done((bf16[128,1024]{1,0:T(8,128)(2,1)S(1)}, bf16[128,1024]{1,0:T(8,128)(2,1)S(1)}, u32[]{:S(2)}, u32[]{:S(2)}) %collective-permute-start.9) | collective-permute-done | bytes 262176 | tf_op jit(solution)/shard_map/ppermute | solution.py:205
  126.1 1.0 fusion.28
  (40 shorter events, 0.5 us)
Async XLA Ops:
  0.6 36.5 %copy-start.8 = (bf16[128,1024]{1,0:T(8,128)(2,1)S(1)}, bf16[128,1024]{1,0:T(8,128)(2,1)}, u32[]{:S(2)}) copy-start(bf16[128,1024]{1,0:T(8,128)(2,1)} %refs_3_.1) | copy-start | bytes 786436
  2.9 20.1 %all-to-all-start.1 = ((bf16[8,32,1024]{2,1,0:T(8,128)(2,1)}), bf16[8,32,1024]{2,1,0:T(8,128)(2,1)S(1)}, u32[]{:S(2)}, u32[]{:S(2)}) async-start(bf16[8,32,1024]{2,1,0:T(8,128)(2,1)} %slots.4), calls=%async_computation.1 | async-start | bytes 1048576 | tf_op jit(solution)/shard_map/all_to_all | solution.py:211
  8.1 12.4 %collective-permute-start.2 = (bf16[128,1024]{1,0:T(8,128)(2,1)}, bf16[128,1024]{1,0:T(8,128)(2,1)S(1)}, u32[]{:S(2)}, u32[]{:S(2)}) collective-permute-start(bf16[128,1024]{1,0:T(8,128)(2,1)} %refs_2_.1), channel_id=1, source_target_pairs={{0,24},{2,26},{4,28},{6,30},{8,16},{10,18},{12,20},{14,22},{16,8},... | collective-permute-start | bytes 786440 | tf_op jit(solution)/shard_map/ppermute | solution.py:205
  10.6 9.9 %collective-permute-start = (f32[4,128]{1,0:T(4,128)S(1)}, f32[4,128]{1,0:T(4,128)S(1)}, u32[]{:S(2)}, u32[]{:S(2)}) collective-permute-start(f32[4,128]{1,0:T(4,128)S(1)} %pad_maximum_fusion.2), channel_id=1, source_target_pairs={{0,24},{2,26},{4,28},{6,30},{8,16},{10,18},{12,20},{14,22},{16,8},... | collective-permute-start | bytes 6152 | tf_op jit(solution)/shard_map/ppermute | solution.py:205
  20.5 0.6 copy-start.10
  22.9 14.2 %all-to-all-start.2 = ((bf16[8,32,1024]{2,1,0:T(8,128)(2,1)}), bf16[8,32,1024]{2,1,0:T(8,128)(2,1)S(1)}, u32[]{:S(2)}, u32[]{:S(2)}) async-start(bf16[8,32,1024]{2,1,0:T(8,128)(2,1)} %slots.5), calls=%async_computation.2 | async-start | bytes 1048576 | tf_op jit(solution)/shard_map/all_to_all | solution.py:211
  29.9 28.0 %collective-permute-start.3 = (bf16[256,1024]{1,0:T(8,128)(2,1)S(1)}, bf16[256,1024]{1,0:T(8,128)(2,1)S(1)}, u32[]{:S(2)}, u32[]{:S(2)}) collective-permute-start(bf16[256,1024]{1,0:T(8,128)(2,1)S(1)} %bitcast.75), channel_id=1, source_target_pairs={{1,0},{0,1},{3,2},{2,3},{5,4},{4,5},{7,6},{6,7},{9,8},{8,9},{11,10... | collective-permute-start | bytes 1572872 | tf_op jit(solution)/shard_map/ppermute | solution.py:218
  37.1 20.8 %collective-permute-start.4 = (bf16[256,1024]{1,0:T(8,128)(2,1)S(1)}, bf16[256,1024]{1,0:T(8,128)(2,1)S(1)}, u32[]{:S(2)}, u32[]{:S(2)}) collective-permute-start(bf16[256,1024]{1,0:T(8,128)(2,1)S(1)} %bitcast.77), channel_id=1, source_target_pairs={{1,0},{0,1},{3,2},{2,3},{5,4},{4,5},{7,6},{6,7},{9,8},{8,9},{11,10... | collective-permute-start | bytes 1572872 | tf_op jit(solution)/shard_map/ppermute | solution.py:218
  37.1 14.3 %collective-permute-start.1 = (bf16[128,1024]{1,0:T(8,128)(2,1)S(1)}, bf16[128,1024]{1,0:T(8,128)(2,1)S(1)}, u32[]{:S(2)}, u32[]{:S(2)}) collective-permute-start(bf16[128,1024]{1,0:T(8,128)(2,1)S(1)} %copy-done.8), channel_id=1, source_target_pairs={{0,24},{2,26},{4,28},{6,30},{8,16},{10,18},{12,20},{14,22},{16,8},... | collective-permute-start | bytes 786440 | tf_op jit(solution)/shard_map/ppermute | solution.py:205
  54.1 17.8 %all-to-all-start = ((bf16[8,64,1024]{2,1,0:T(8,128)(2,1)}), bf16[8,64,1024]{2,1,0:T(8,128)(2,1)S(1)}, u32[]{:S(2)}, u32[]{:S(2)}) async-start(bf16[8,64,1024]{2,1,0:T(8,128)(2,1)} %slots.3), calls=%async_computation | async-start | bytes 2097152 | tf_op jit(solution)/shard_map/all_to_all | solution.py:211
  58.0 2.2 %copy-start.3 = (bf16[1,2048,1024]{2,1,0:T(8,128)(2,1)S(1)}, bf16[1,2048,1024]{2,1,0:T(8,128)(2,1)}, u32[]{:S(2)}) copy-start(bf16[1,2048,1024]{2,1,0:T(8,128)(2,1)} %param.11) | copy-start | bytes 12582916
  60.2 2.3 %copy-start.11 = (bf16[1,2048,1024]{2,1,0:T(8,128)(2,1)S(1)}, bf16[1,2048,1024]{2,1,0:T(8,128)(2,1)}, u32[]{:S(2)}) copy-start(bf16[1,2048,1024]{2,1,0:T(8,128)(2,1)} %param.10) | copy-start | bytes 12582916
  62.5 4.1 %copy-start.6 = (bf16[1024,1024]{1,0:T(8,128)(2,1)S(1)}, bf16[1024,1024]{1,0:T(8,128)(2,1)}, u32[]{:S(2)}) copy-start(bf16[1024,1024]{1,0:T(8,128)(2,1)} %get-tuple-element.16) | copy-start | bytes 6291460
  66.6 1.4 %copy-start.14 = (bf16[512,1024]{1,0:T(8,128)(2,1)}, bf16[512,1024]{1,0:T(8,128)(2,1)S(1)}, u32[]{:S(2)}) copy-start(bf16[512,1024]{1,0:T(8,128)(2,1)S(1)} %get-tuple-element.14.refs_2_) | copy-start | bytes 3145732
  66.6 2.0 %copy-start.5 = (bf16[1024,1024]{1,0:T(8,128)(2,1)S(1)}, bf16[1024,1024]{1,0:T(8,128)(2,1)}, u32[]{:S(2)}) copy-start(bf16[1024,1024]{1,0:T(8,128)(2,1)} %get-tuple-element.15) | copy-start | bytes 6291460
  67.9 2.7 %collective-permute-start.5 = (bf16[512,1024]{1,0:T(8,128)(2,1)S(1)}, bf16[512,1024]{1,0:T(8,128)(2,1)S(1)}, u32[]{:S(2)}, u32[]{:S(2)}) collective-permute-start(bf16[512,1024]{1,0:T(8,128)(2,1)S(1)} %convolution_convert_fusion), channel_id=1, source_target_pairs={{0,1},{1,0},{2,3},{3,2},{4,5},{5,4},{6,7},{7,6},{8,9},{9,8},{10,11... | collective-permute-start | bytes 3145736 | tf_op jit(solution)/shard_map/ppermute | solution.py:224
  72.0 7.7 %copy-start = (bf16[8,64,1024]{2,1,0:T(8,128)(2,1)}, bf16[8,64,1024]{2,1,0:T(8,128)(2,1)S(1)}, u32[]{:S(2)}) copy-start(bf16[8,64,1024]{2,1,0:T(8,128)(2,1)S(1)} %all-to-all-done) | copy-start | bytes 3145732
  72.0 5.0 %collective-permute-start.7 = (bf16[512,1024]{1,0:T(8,128)(2,1)S(1)}, bf16[512,1024]{1,0:T(8,128)(2,1)}, u32[]{:S(2)}, u32[]{:S(2)}) collective-permute-start(bf16[512,1024]{1,0:T(8,128)(2,1)S(1)} %bitcast.70), channel_id=1, source_target_pairs={{1,0},{0,1},{3,2},{2,3},{5,4},{4,5},{7,6},{6,7},{9,8},{8,9},{11,10... | collective-permute-start | bytes 3145736 | tf_op jit(solution)/shard_map/ppermute | solution.py:218
  72.1 19.3 %all-to-all-start.3 = ((bf16[8,64,1024]{2,1,0:T(8,128)(2,1)}), bf16[8,64,1024]{2,1,0:T(8,128)(2,1)S(1)}, u32[]{:S(2)}, u32[]{:S(2)}) async-start(bf16[8,64,1024]{2,1,0:T(8,128)(2,1)} %bitcast.15), calls=%async_computation.3 | async-start | bytes 2097152 | tf_op jit(solution)/shard_map/all_to_all | solution.py:211
  77.0 2.7 %copy-start.1 = (bf16[1,1024,2048]{2,1,0:T(8,128)(2,1)S(1)}, bf16[1,1024,2048]{2,1,0:T(8,128)(2,1)}, u32[]{:S(2)}) copy-start(bf16[1,1024,2048]{2,1,0:T(8,128)(2,1)} %param.12) | copy-start | bytes 12582916
  79.7 2.4 %copy-start.4 = (bf16[1,2048,1024]{2,1,0:T(8,128)(2,1)S(1)}, bf16[1,2048,1024]{2,1,0:T(8,128)(2,1)}, u32[]{:S(2)}) copy-start(bf16[1,2048,1024]{2,1,0:T(8,128)(2,1)} %param.11) | copy-start | bytes 12582916
  82.0 2.2 %copy-start.12 = (bf16[1,2048,1024]{2,1,0:T(8,128)(2,1)S(1)}, bf16[1,2048,1024]{2,1,0:T(8,128)(2,1)}, u32[]{:S(2)}) copy-start(bf16[1,2048,1024]{2,1,0:T(8,128)(2,1)} %param.10) | copy-start | bytes 12582916
  82.1 2.5 %copy-start.13 = (bf16[512,1024]{1,0:T(8,128)(2,1)S(1)}, bf16[512,1024]{1,0:T(8,128)(2,1)}, u32[]{:S(2)}) copy-start(bf16[512,1024]{1,0:T(8,128)(2,1)} %get-tuple-element.22) | copy-start | bytes 3145732
  85.8 2.7 %collective-permute-start.8 = (bf16[512,1024]{1,0:T(8,128)(2,1)S(1)}, bf16[512,1024]{1,0:T(8,128)(2,1)S(1)}, u32[]{:S(2)}, u32[]{:S(2)}) collective-permute-start(bf16[512,1024]{1,0:T(8,128)(2,1)S(1)} %add_convert_fusion.1), channel_id=1, source_target_pairs={{0,1},{1,0},{2,3},{3,2},{4,5},{5,4},{6,7},{7,6},{8,9},{9,8},{10,11... | collective-permute-start | bytes 3145736 | tf_op jit(solution)/shard_map/ppermute | solution.py:224
  91.5 5.7 %copy-start.2 = (bf16[8,64,1024]{2,1,0:T(8,128)(2,1)}, bf16[8,64,1024]{2,1,0:T(8,128)(2,1)S(1)}, u32[]{:S(2)}) copy-start(bf16[8,64,1024]{2,1,0:T(8,128)(2,1)S(1)} %all-to-all-done.3.refs_3_) | copy-start | bytes 3145732
  91.5 18.2 %all-to-all-start.4 = ((bf16[8,64,1024]{2,1,0:T(8,128)(2,1)}), bf16[8,64,1024]{2,1,0:T(8,128)(2,1)S(1)}, u32[]{:S(2)}, u32[]{:S(2)}) async-start(bf16[8,64,1024]{2,1,0:T(8,128)(2,1)} %bitcast.22), calls=%async_computation.4 | async-start | bytes 2097152 | tf_op jit(solution)/shard_map/all_to_all | solution.py:211
  100.1 18.5 %collective-permute-start.6 = (bf16[128,1024]{1,0:T(8,128)(2,1)}, bf16[128,1024]{1,0:T(8,128)(2,1)S(1)}, u32[]{:S(2)}, u32[]{:S(2)}) collective-permute-start(bf16[128,1024]{1,0:T(8,128)(2,1)} %get-tuple-element.19), channel_id=1, source_target_pairs={{0,24},{2,26},{4,28},{6,30},{8,16},{10,18},{12,20},{14,22},{16,8},... | collective-permute-start | bytes 786440 | tf_op jit(solution)/shard_map/ppermute | solution.py:205
  110.9 15.3 %collective-permute-start.9 = (bf16[128,1024]{1,0:T(8,128)(2,1)S(1)}, bf16[128,1024]{1,0:T(8,128)(2,1)S(1)}, u32[]{:S(2)}, u32[]{:S(2)}) collective-permute-start(bf16[128,1024]{1,0:T(8,128)(2,1)S(1)} %fusion.29), channel_id=1, source_target_pairs={{0,24},{2,26},{4,28},{6,30},{8,16},{10,18},{12,20},{14,22},{16,8},... | collective-permute-start | bytes 786440 | tf_op jit(solution)/shard_map/ppermute | solution.py:205
  112.4 6.2 %copy-start.7 = (f32[128,1024]{1,0:T(8,128)S(1)}, f32[128,1024]{1,0:T(8,128)}, u32[]{:S(2)}) copy-start(f32[128,1024]{1,0:T(8,128)} %get-tuple-element.18) | copy-start | bytes 1572868
  112.4 13.7 %copy-start.9 = (bf16[8,64,128]{2,1,0:T(8,128)(2,1)S(1)}, bf16[8,64,128]{2,1,0:T(8,128)(2,1)}, u32[]{:S(2)}) copy-start(bf16[8,64,128]{2,1,0:T(8,128)(2,1)} %get-tuple-element.20) | copy-start | bytes 393220
